TPU v7x, 32 devices: a whole 2x2x4 slice. The times are simulated.
32 devices in a mesh: dp: 8 (over z, y), tensor: 4 (over x, core).
Axes of the slice: x: 2, y: 2, z: 4, core: 2. Of those that a mesh axis runs over, the one named last changes fastest.
Arguments:
- frames: bfloat16 [8, 1024, 768], P('dp'), may hold values from -6 to 6
- frame_mask: int32 [8, 1024], P('dp'), may hold values from 0 to 1, as said below
- mask_embedding: float32 [768], replicated, may hold values from -6 to 6
- query_weight: bfloat16 [768, 768], P(None, 'tensor'), may hold values from -0.21875 to 0.21875
- query_bias: float32 [768], P('tensor'), may hold values from -3 to 3
- key_weight: bfloat16 [768, 768], P(None, 'tensor'), may hold values from -0.21875 to 0.21875
- value_weight: bfloat16 [768, 768], P(None, 'tensor'), may hold values from -0.21875 to 0.21875
- value_bias: float32 [768], P('tensor'), may hold values from -3 to 3
- out_weight: bfloat16 [768, 768], P('tensor'), may hold values from -0.625 to 0.625
- out_bias: float32 [768], replicated, may hold values from -3 to 3
- norm1_gain: float32 [768], replicated, may hold values from 0.5 to 1.5
- norm1_shift: float32 [768], replicated, may hold values from -3 to 3
- up_weight: bfloat16 [768, 3072], P(None, 'tensor'), may hold values from -0.21875 to 0.21875
- up_bias: float32 [3072], P('tensor'), may hold values from -3 to 3
- down_weight: bfloat16 [3072, 768], P('tensor'), may hold values from -0.109375 to 0.109375
- down_bias: float32 [768], replicated, may hold values from -3 to 3
- norm2_gain: float32 [768], replicated, may hold values from 0.5 to 1.5
- norm2_shift: float32 [768], replicated, may hold values from -3 to 3
- cotangent: bfloat16 [8, 1024, 768], P('dp'), may hold values from -6 to 6
Outputs:
- output: bfloat16 [8, 1024, 768], P('dp')
- frames_grad: bfloat16 [8, 1024, 768], P('dp')
- mask_embedding_grad: float32 [768], replicated
- query_weight_grad: float32 [768, 768], P(None, 'tensor')
- query_bias_grad: float32 [768], P('tensor')
- key_weight_grad: float32 [768, 768], P(None, 'tensor')
- value_weight_grad: float32 [768, 768], P(None, 'tensor')
- value_bias_grad: float32 [768], P('tensor')
- out_weight_grad: float32 [768, 768], P('tensor')
- out_bias_grad: float32 [768], replicated
- norm1_gain_grad: float32 [768], replicated
- norm1_shift_grad: float32 [768], replicated
- up_weight_grad: float32 [768, 3072], P(None, 'tensor')
- up_bias_grad: float32 [3072], P('tensor')
- down_weight_grad: float32 [3072, 768], P('tensor')
- down_bias_grad: float32 [768], replicated
- norm2_gain_grad: float32 [768], replicated
- norm2_shift_grad: float32 [768], replicated
Inputs may be any that keep to these rules, and one draw needn't show every extreme that they name: `frame_mask`: 1 marks a frame inside one of 68 spans of 10 frames whose starts are drawn for each clip; spans may intersect.
All inputs are finite; a program needn't handle non-finite values.
Results may differ from a plain program's by a relative error of at most 0.017.
Values sent between devices are 32-bit elements; how exact they have to be, the bound alone decides.
No kernel may reach another device: no remote copies, remote signals or barrier semaphores. Data moves between devices by JAX's collectives and lax.ppermute only.
A program may use at most 128 MiB of HBM per device.

v0:
```python
import math

import jax
import jax.numpy as jnp
from jax import lax
from jax.experimental import pallas as pl
from jax.experimental.pallas import tpu as pltpu
from jax.sharding import PartitionSpec as P

HEAD = 64
AXES = ("dp", "tensor")
STEPS = 2
TURNS = (True, True, True)
ORDER = (
    "Dk", "Ds", "Uk", "N0", "Us", "D1", "U1", "N1", "D2", "U2", "at", "tk", "D3", "ts", "A0",
    "A1", "os", "qk", "T1", "U3", "F0", "D4", "T2", "D5", "F1", "U4", "T3", "V", "U5", "T4",
    "V0", "D6", "V1", "T5", "U6", "V2", "T6",
)


def local_dot(left, right):
    return jnp.dot(left, right, preferred_element_type=jnp.float32)


def dot_rows(left, right):
    return lax.dot_general(
        left, right, (((0,), (0,)), ((), ())), preferred_element_type=jnp.float32
    )


def dot_trans(left, right):
    return lax.dot_general(
        left, right, (((1,), (1,)), ((), ())), preferred_element_type=jnp.float32
    )


def normalize(values):
    centered = values - jnp.mean(values, -1, keepdims=True)
    inverse = lax.rsqrt(jnp.mean(centered * centered, -1, keepdims=True) + 1e-05)
    return (centered * inverse, inverse)


def norm_backward(grad_normed, normed, inverse):
    return inverse * (
        grad_normed
        - jnp.mean(grad_normed, -1, keepdims=True)
        - normed * jnp.mean(grad_normed * normed, -1, keepdims=True)
    )


class Swaps:
    def __init__(self, mesh):
        self.dp = mesh.shape["dp"]
        self.tensor = mesh.shape["tensor"]
        index = lax.axis_index("dp")
        self.masks = [1 << bit for bit in range(self.dp.bit_length() - 1)]
        self.coords = [(index >> bit) & 1 for bit in range(len(self.masks))]
        self.core = lax.axis_index("tensor") % 2

    def move(self, value, target):
        pairs = []
        for row in range(self.dp):
            for column in range(self.tensor):
                to_row, to_column = target(row, column)
                pairs.append((row * self.tensor + column, to_row * self.tensor + to_column))
        return lax.ppermute(value, AXES, pairs)

    def over_core(self, value):
        return self.move(value, lambda row, column: (row, column ^ 1))

    def over_chip(self, value):
        return self.move(value, lambda row, column: (row, column ^ 2))

    def over_dp(self, value, even, odd):
        masks = self.masks
        return self.move(
            value, lambda row, column: (row ^ masks[odd if column % 2 else even], column)
        )

    def plan(self, turn):
        steps = list(range(len(self.masks)))
        turned = steps[1::-1] + steps[2:] if turn else steps
        result = []
        for even, odd in zip(steps, turned):
            coord = jnp.where(self.core == 0, self.coords[even], self.coords[odd])
            result.append((even, odd, coord))
        return result


class Order:
    def __init__(self):
        self.last = ()

    def begin(self, *arrays):
        arrays, _ = lax.optimization_barrier((arrays, self.last))
        self.last = ()
        return arrays[0] if len(arrays) == 1 else arrays

    def end(self, *arrays):
        self.last += arrays
        return arrays[0] if len(arrays) == 1 else arrays


class Total:
    def __init__(self, swaps, order, turn):
        self.swaps, self.order, self.plan = swaps, order, swaps.plan(turn)
        self.queue = [self.first] + [self.halve] * (len(self.plan) - 2)
        self.queue += [self.exchange, self.settle] + [self.double] * (len(self.plan) - 1)

    def load(self, value, got=None):
        self.keep, self.got, self.at = value, got, -1
        self.queue.pop(0) if got is None else None
        if got is None:
            self.first()
        else:
            self.queue[0] = self.halve
            self.advance()

    def advance(self, count=1):
        for _ in range(count):
            if self.queue:
                self.queue.pop(0)()

    def send(self, value):
        even, odd, _ = self.plan[self.at]
        self.got = self.swaps.over_dp(value, even, odd)

    def first(self):
        self.at = 0
        coord = self.plan[0][2]
        rows = self.keep.shape[0] // 2
        value = self.order.begin(self.keep)
        self.send(self.order.end(pick(value, 1 - coord, rows)))
        self.keep = pick(value, coord, rows)

    def halve(self):
        self.at += 1
        coord = self.plan[self.at][2]
        rows = self.keep.shape[0] // 2
        keep, got = self.order.begin(self.keep, self.got)
        send = pick(keep, 1 - coord, rows) + pick(got, 1 - coord, rows)
        self.keep = pick(keep, coord, rows) + pick(got, coord, rows)
        self.order.end(send, self.keep)
        self.send(send)

    def exchange(self):
        self.at += 1
        keep, got = self.order.begin(self.keep, self.got)
        self.keep = self.order.end(keep + got)
        self.send(self.keep)

    def settle(self):
        keep, got = self.order.begin(self.keep, self.got)
        self.keep = self.order.end(keep + got)
        self.at -= 1
        self.send(self.keep)

    def double(self):
        first = self.plan[self.at][2] == 0
        keep, got = self.order.begin(self.keep, self.got)
        self.keep = self.order.end(
            jnp.concatenate([jnp.where(first, keep, got), jnp.where(first, got, keep)], 0)
        )
        self.at -= 1
        if self.at >= 0:
            self.send(self.keep)

    def finish(self):
        self.advance(len(self.queue))
        return self.keep


VMEM = pl.BlockSpec(memory_space=pltpu.VMEM)
SMEM = pl.BlockSpec(memory_space=pltpu.SMEM)


def kernel_call(body, outputs, *arrays, **options):
    shapes = [jax.ShapeDtypeStruct(shape, kind) for shape, kind in outputs]
    options.setdefault("in_specs", [VMEM] * len(arrays))
    options.setdefault("out_specs", [VMEM] * len(shapes))
    return pl.pallas_call(
        body,
        out_shape=shapes,
        cost_estimate=pl.CostEstimate(flops=1, bytes_accessed=1, transcendentals=0),
        compiler_params=pltpu.CompilerParams(vmem_limit_bytes=24 * 1024 * 1024),
        **options,
    )(*arrays)


def send_body(context, send_out, own_out):
    rows = send_out.shape[0]
    send_out[...] = context[rows:].astype(jnp.float32) * 2.0
    own_out[...] = context[:rows].astype(jnp.float32) * 2.0


def pack_body(own, pair, *outs):
    *steps, chip_out = outs
    rows, width = steps[0].shape[0], own.shape[1]
    for index, out in enumerate(steps):
        at = slice(index * rows, (index + 1) * rows)
        out[:, :width] = own[at]
        out[:, width:] = pair[at]
        chip_out[at, :width] = (own[at] * 0.5).astype(jnp.bfloat16)
        chip_out[at, width:] = (pair[at] * 0.5).astype(jnp.bfloat16)


def join_body(
    index, up, up_pair, down, down_pair, bias, bias_pair, out_all,
    up_out, down_out, bias_out, chip_out, other_out,
):
    width = up.shape[1]
    up_out[:, :width] = up[...]
    up_out[:, width:] = (up_pair[...] * 0.5).astype(jnp.bfloat16)
    down_out[:width] = down[...]
    down_out[width:] = (down_pair[...] * 0.5).astype(jnp.bfloat16)
    bias_out[:, :width] = bias[...]
    bias_out[:, width:] = bias_pair[...]
    rows = chip_out.shape[0] // 2
    for mask, out in enumerate((chip_out, chip_out, other_out, other_out)):
        at = pl.ds(pl.multiple_of((index[0] ^ mask) * rows, 8), rows)
        to = slice(mask % 2 * rows, (mask % 2 + 1) * rows)
        out[to] = (out_all[at] * 0.5).astype(jnp.bfloat16)


def second_body(
    hidden, part, got, cotangent, slope, down, up, bias, gain,
    normed_out, grad_out, low_out, units_out, part_out, sums_out, wide_out,
):
    rows = hidden.shape[0] // 2
    sums_out[...] = jnp.zeros_like(sums_out)
    wide_out[...] = jnp.zeros_like(wide_out)

    def one(block, carry):
        at = pl.ds(pl.multiple_of(block * rows, 8), rows)
        normed, inverse = normalize(hidden[at] + (part[at] + got[at]) + bias[...])
        normed_out[at] = normed
        grad = cotangent[at].astype(jnp.float32)
        sums_out[0:1] += jnp.sum(grad * normed, 0, keepdims=True)
        sums_out[1:2] += jnp.sum(grad, 0, keepdims=True)
        grad = norm_backward(grad * gain[...], normed, inverse)
        grad_out[at] = grad
        sums_out[2:3] += jnp.sum(grad, 0, keepdims=True)
        low = grad.astype(jnp.bfloat16)
        low_out[at] = low
        units = (dot_trans(low, down[...]) * slope[at]).astype(jnp.bfloat16)
        units_out[at] = units
        wide_out[...] += jnp.sum(units.astype(jnp.float32), 0, keepdims=True)
        part_out[at] = dot_trans(units, up[...])
        return carry

    lax.fori_loop(0, 2, one, 0)


def first_body(
    grad_two, part, got, normed, inverse, gain, own, pair,
    grad_out, low_out, wide_out, own_out, sums_out,
):
    rows = part.shape[0] // 2
    sums_out[...] = jnp.zeros_like(sums_out)

    def one(block, carry):
        at = pl.ds(pl.multiple_of(block * rows, 8), rows)
        grad = grad_two[at] + (part[at] + got[at])
        sums_out[0:1] += jnp.sum(grad * normed[at], 0, keepdims=True)
        sums_out[1:2] += jnp.sum(grad, 0, keepdims=True)
        grad = norm_backward(grad * gain[...], normed[at], inverse[at])
        grad_out[at] = grad
        sums_out[2:3] += jnp.sum(grad, 0, keepdims=True)
        low = grad.astype(jnp.bfloat16)
        low_out[at] = low
        own_out[at] = dot_trans(low, own[...]).astype(jnp.bfloat16)
        turned = dot_trans(low, pair[...]).astype(jnp.bfloat16)
        wide_out[at] = turned.astype(jnp.float32) * 2.0
        return carry

    lax.fori_loop(0, 2, one, 0)


def attention_back_body(query, keys, values, sums, grads, keys_turned, query_out, keys_out, values_out):
    length = query.shape[1]
    rows = min(256, length)
    scale = 1.0 / math.sqrt(HEAD)
    key_rows, value_rows, turned = keys[0], values[0], keys_turned[0]
    key_sum = jnp.zeros((length, HEAD), jnp.float32)
    value_sum = jnp.zeros((length, HEAD), jnp.float32)
    for block in range(length // rows):
        at = pl.ds(block * rows, rows)
        asked, grad = query[0, at], grads[0, at]
        attn = jnp.exp(dot_trans(key_rows, asked) * scale - sums[0, :, at])
        value_sum += local_dot(attn.astype(jnp.bfloat16), grad)
        grad_attn = dot_trans(value_rows, grad)
        mean = jnp.sum(attn * grad_attn, 0, keepdims=True)
        scores = (attn * (grad_attn - mean)).astype(jnp.bfloat16)
        key_sum += local_dot(scores, asked)
        query_out[0, :, at] = (local_dot(turned, scores) * scale).astype(jnp.bfloat16)
    keys_out[0] = (key_sum * scale).astype(jnp.bfloat16)
    values_out[0] = value_sum.astype(jnp.bfloat16)


def pick(block, part, rows):
    return lax.dynamic_slice_in_dim(block, part * rows, rows, 0)


def widen(array):
    return array.astype(jnp.float32) * 2.0


def narrow(array):
    return (array * 0.5).astype(jnp.bfloat16)


def shards(
    mesh,
    frames,
    frame_mask,
    mask_embedding,
    query_weight,
    query_bias,
    key_weight,
    value_weight,
    value_bias,
    out_weight,
    out_bias,
    norm1_gain,
    norm1_shift,
    up_weight,
    up_bias,
    down_weight,
    down_bias,
    norm2_gain,
    norm2_shift,
    cotangent,
):
    swaps = Swaps(mesh)
    order = Order()
    clip_count, length, model_width = frames.shape
    token_rows = clip_count * length
    local_width = query_weight.shape[1]
    heads_here = local_width // HEAD
    score_scale = 1.0 / math.sqrt(HEAD)
    head_shape = (clip_count, length, heads_here, HEAD)
    own_rows = token_rows // 2
    step_rows = own_rows // STEPS
    core = swaps.core
    tensor_index = lax.axis_index("tensor")

    def step(array, k):
        return array[k * step_rows : (k + 1) * step_rows]

    out_all = lax.all_gather(widen(out_weight), "tensor", tiled=True)
    up_wide, down_wide = widen(up_weight), widen(down_weight)
    up_pair = swaps.over_core(up_wide)
    down_pair = swaps.over_core(down_wide)
    order.end(up_wide, down_wide)
    up_bias_row = up_bias.reshape(1, -1)
    up_bias_pair = swaps.over_core(up_bias_row)

    def masked(part):
        rows = pick(frame_mask.reshape(token_rows, 1), part, own_rows).astype(jnp.float32)
        block = pick(frames.reshape(token_rows, model_width), part, own_rows)
        return block.astype(jnp.float32) * (1.0 - rows) + rows * mask_embedding, rows

    masked_in, masked_rows = masked(core)
    masked_low = jnp.concatenate(
        [masked_in.astype(jnp.bfloat16), masked(1 - core)[0].astype(jnp.bfloat16)], 0
    )
    grad_out = pick(cotangent.reshape(token_rows, model_width), core, own_rows)
    masked_low = order.begin(masked_low)
    query = (local_dot(masked_low, query_weight) + query_bias).astype(jnp.bfloat16)
    keys = local_dot(masked_low, key_weight).astype(jnp.bfloat16)
    values = (local_dot(masked_low, value_weight) + value_bias).astype(jnp.bfloat16)
    query_heads = query.reshape(head_shape)
    key_heads = keys.reshape(head_shape)
    value_heads = values.reshape(head_shape)
    scores = (
        jnp.einsum("cqhd,ckhd->chqk", query_heads, key_heads, preferred_element_type=jnp.float32)
        * score_scale
    )
    row_max = jnp.max(scores, -1, keepdims=True)
    expo = jnp.exp(scores - row_max)
    totals = jnp.sum(expo, -1, keepdims=True)
    log_sum = row_max + jnp.log(totals)
    attn_low = (expo / totals).astype(jnp.bfloat16)
    context = jnp.einsum(
        "chqk,ckhd->cqhd", attn_low, value_heads, preferred_element_type=jnp.float32
    )
    context = context.reshape(token_rows, local_width).astype(jnp.bfloat16)

    narrow_half = (own_rows, local_width)
    context_send, context_own = kernel_call(
        send_body, [(narrow_half, jnp.float32)] * 2, order.begin(context)
    )
    order.end(context_send)
    context_pair = swaps.over_core(context_send)
    chip_step = (step_rows, 2 * local_width)
    *chip_steps, context_chip = kernel_call(
        pack_body,
        [(chip_step, jnp.float32)] * STEPS + [((own_rows, chip_step[1]), jnp.bfloat16)],
        *order.begin(context_own, context_pair),
    )
    order.end(*chip_steps, context_chip)
    other_wide = [swaps.over_chip(block) for block in chip_steps]
    out_all, up_pair, down_pair = order.begin(out_all, up_pair, down_pair)
    units_here = up_weight.shape[1]
    operands = (
        tensor_index.reshape(1),
        up_weight,
        up_pair,
        down_weight,
        down_pair,
        up_bias_row,
        up_bias_pair,
        out_all,
    )
    up_chip, down_chip, up_bias_chip, out_chip, out_other = kernel_call(
        join_body,
        [
            ((model_width, 2 * units_here), jnp.bfloat16),
            ((2 * units_here, model_width), jnp.bfloat16),
            ((1, 2 * units_here), jnp.float32),
            ((2 * local_width, model_width), jnp.bfloat16),
            ((2 * local_width, model_width), jnp.bfloat16),
        ],
        *operands,
        in_specs=[SMEM] + [VMEM] * 7,
    )
    out_parts = [out_chip[:local_width], out_chip[local_width:]]
    order.end(out_chip, out_other, up_chip, down_chip)

    normed_one, inverse_one, ffn_in, activ, slope = [], [], [], [], []
    hidden_one, ffn_part, ffn_got = [], [], []
    for k in range(STEPS):
        rows, wide = order.begin(step(context_chip, k), other_wide[k])
        attended = local_dot(rows, out_chip) + local_dot(narrow(wide), out_other)
        normed, inverse = normalize(step(masked_in, k) + attended + out_bias)
        hidden = normed * norm1_gain + norm1_shift
        low = hidden.astype(jnp.bfloat16)
        pre_act = local_dot(low, up_chip) + up_bias_chip
        normal_cdf = 0.5 * (1.0 + lax.erf(pre_act / math.sqrt(2.0)))
        normal_pdf = jnp.exp(-0.5 * pre_act * pre_act) / math.sqrt(2.0 * math.pi)
        units = (pre_act * normal_cdf).astype(jnp.bfloat16)
        part = order.end(local_dot(units, down_chip))
        ffn_part.append(part)
        ffn_got.append(swaps.over_chip(part))
        normed_one.append(normed)
        inverse_one.append(inverse)
        hidden_one.append(hidden)
        ffn_in.append(low)
        activ.append(units)
        slope.append(normal_cdf + pre_act * normal_pdf)

    def by_head(array):
        split = array.reshape(clip_count, length, heads_here, HEAD)
        return split.transpose(0, 2, 1, 3).reshape(clip_count * heads_here, length, HEAD)

    query, keys, values = order.begin(query, keys, values)
    keys_by_head = by_head(keys)
    attention_operands = order.end(
        by_head(query),
        keys_by_head,
        by_head(values),
        log_sum.reshape(clip_count * heads_here, 1, length),
        keys_by_head.transpose(0, 2, 1),
    )
    output, grad_h2, grad_h2_low, grad_pre, one_part, one_got = [], [], [], [], [], []
    gain_two, shift_two, bias_down, bias_up = [], [], [], []
    for k in range(STEPS):
        part, got = order.begin(ffn_part[k], ffn_got[k])
        square, wide = (step_rows, model_width), (step_rows, 2 * units_here)
        normed, grad_two, low, units, part, sums, unit_sums = kernel_call(
            second_body,
            [
                (square, jnp.float32),
                (square, jnp.float32),
                (square, jnp.bfloat16),
                (wide, jnp.bfloat16),
                (square, jnp.float32),
                ((3, model_width), jnp.float32),
                ((1, 2 * units_here), jnp.float32),
            ],
            hidden_one[k],
            part,
            got,
            step(grad_out, k),
            slope[k],
            down_chip,
            up_chip,
            down_bias[None],
            norm2_gain[None],
        )
        order.end(part)
        output.append(normed)
        gain_two.append(sums[0])
        shift_two.append(sums[1])
        bias_down.append(sums[2])
        bias_up.append(unit_sums[0])
        one_part.append(part)
        one_got.append(swaps.over_chip(part))
        grad_h2.append(grad_two)
        grad_h2_low.append(low)
        grad_pre.append(units)

    activ = jnp.concatenate(activ, 0)
    ffn_in = jnp.concatenate(ffn_in, 0)
    grad_h2_low = jnp.concatenate(grad_h2_low, 0)
    grad_pre = jnp.concatenate(grad_pre, 0)
    totals = {name: Total(swaps, order, turn) for name, turn in zip("DUT", TURNS)}
    v = {}
    heads = clip_count * heads_here
    rows = own_rows // 2

    def by_row(array):
        split = array.reshape(clip_count, heads_here, length, HEAD)
        return split.transpose(0, 2, 1, 3).reshape(token_rows, local_width)

    def weight_grad(left, right):
        return order.end(dot_rows(*order.begin(left, right)))

    def down_send():
        send = weight_grad(activ[:, units_here:], grad_h2_low)
        v["down_got"] = swaps.over_core(send)

    def down_keep():
        v["down"] = weight_grad(activ[:, :units_here], grad_h2_low)

    def up_send():
        send = weight_grad(ffn_in, grad_pre[:, units_here:])
        v["up_got"] = swaps.over_core(send)

    def up_keep():
        v["up"] = weight_grad(ffn_in, grad_pre[:, :units_here])

    def first_norm(k):
        part, got = order.begin(one_part[k], one_got[k])
        square, narrow_shape = (step_rows, model_width), (step_rows, local_width)
        v["one", k] = kernel_call(
            first_body,
            [
                (square, jnp.float32),
                (square, jnp.bfloat16),
                (narrow_shape, jnp.float32),
                (narrow_shape, jnp.bfloat16),
                ((3, model_width), jnp.float32),
            ],
            grad_h2[k],
            part,
            got,
            normed_one[k],
            inverse_one[k],
            norm1_gain[None],
            out_parts[0],
            out_parts[1],
        )
        order.end(v["one", k][2], v["one", k][3])
        if k == STEPS - 1:
            kernels = [v["one", at] for at in range(STEPS)]
            v["context_got"] = swaps.over_core(jnp.concatenate([one[2] for one in kernels], 0))
            v["context_own"] = [one[3] for one in kernels]
            v["h1_low"] = jnp.concatenate([one[1] for one in kernels], 0)
            v["h1"] = jnp.concatenate([one[0] for one in kernels], 0)

    def attention():
        grad_context = jnp.concatenate(v["context_own"] + [narrow(v["context_got"])], 0)
        head_block = pl.BlockSpec((1, length, HEAD), lambda head: (head, 0, 0))
        turned_block = pl.BlockSpec((1, HEAD, length), lambda head: (head, 0, 0))
        row_block = pl.BlockSpec((1, 1, length), lambda head: (head, 0, 0))
        operands = attention_operands[:4] + (by_head(grad_context),) + attention_operands[4:]
        grad_query, grad_keys, grad_values = kernel_call(
            attention_back_body,
            [
                ((heads, HEAD, length), jnp.bfloat16),
                ((heads, length, HEAD), jnp.bfloat16),
                ((heads, length, HEAD), jnp.bfloat16),
            ],
            *order.begin(*operands),
            grid=(heads,),
            in_specs=[head_block, head_block, head_block, row_block, head_block, turned_block],
            out_specs=[turned_block, head_block, head_block],
        )
        order.end(grad_query, grad_keys, grad_values)
        v["query"] = by_row(grad_query.transpose(0, 2, 1))
        v["values"] = by_row(grad_values)
        v["three"] = jnp.concatenate([v["query"], by_row(grad_keys), v["values"]], 1)

    attn_weight = jnp.concatenate([query_weight, key_weight, value_weight], 1)

    def terms_send():
        v["three"] = order.begin(v["three"])
        send = order.end(dot_trans(v["three"][own_rows:], attn_weight))
        v["terms_got"] = swaps.over_core(send)

    def terms_keep():
        three = order.begin(v["three"])
        v["terms"] = order.end(dot_trans(three[:own_rows], attn_weight))

    def chip_terms(k):
        at = slice(k * rows, (k + 1) * rows)
        part, got = order.begin(v["terms"][at], v["terms_got"][at])
        v["chip", k] = order.end(part + got)
        v["chip_got", k] = swaps.over_chip(v["chip", k])

    def out_send():
        send = weight_grad(context_chip[:, local_width:], v["h1_low"])
        v["out_got"] = swaps.over_core(send)

    def three_grad():
        v["three_grad"] = weight_grad(v["three"], masked_low)

    def join():
        keep, got = order.begin(
            dot_rows(context_chip[:, :local_width], v["h1_low"]), v["out_got"]
        )
        joined = order.end(jnp.concatenate([v["three_grad"], keep + got], 0))
        totals["T"].load(joined)

    def frames_step(k):
        at = slice(k * rows, (k + 1) * rows)
        part, got = order.begin(v["chip", k], v["chip_got", k])
        grad_in = v["h1"][at] + (part + got)
        v["mask", k] = jnp.sum(grad_in * masked_rows[at], 0)
        v["frames", k] = order.end(grad_in)

    def vectors():
        kernels = [v["one", at][4] for at in range(STEPS)]
        shared = (
            v["mask", 0] + v["mask", 1],
            sum(sums[2] for sums in kernels),
            sum(sums[0] for sums in kernels),
            sum(sums[1] for sums in kernels),
            sum(bias_down),
            sum(gain_two),
            sum(shift_two),
        )
        own_bias_up = sum(bias_up)
        pair = jnp.concatenate(shared + (own_bias_up[units_here:],))[None]
        mine = jnp.concatenate(shared + (own_bias_up[:units_here],))[None]
        mine, pair_got = order.begin(mine, swaps.over_core(pair))
        attention_bias = [
            jnp.sum(v[name].astype(jnp.float32), 0)[None] for name in ("query", "values")
        ]
        v["packed"] = order.end(jnp.concatenate([mine + pair_got] + attention_bias, 1))

    def vector_step(link):
        packed, got = order.begin(v["packed"], swaps.over_dp(v["packed"], link, link))
        v["packed"] = order.end(packed + got)

    stages = {
        "Ds": down_send,
        "Dk": down_keep,
        "Us": up_send,
        "Uk": up_keep,
        "N0": lambda: first_norm(0),
        "N1": lambda: first_norm(1),
        "at": attention,
        "ts": terms_send,
        "tk": terms_keep,
        "A0": lambda: chip_terms(0),
        "A1": lambda: chip_terms(1),
        "os": out_send,
        "qk": three_grad,
        "T1": join,
        "F0": lambda: frames_step(0),
        "F1": lambda: frames_step(1),
        "V": vectors,
        "V0": lambda: vector_step(0),
        "V1": lambda: vector_step(1),
        "V2": lambda: [vector_step(link) for link in range(2, len(swaps.masks))],
        "D1": lambda: totals["D"].load(v["down"], v["down_got"]),
        "U1": lambda: totals["U"].load(v["up"], v["up_got"]),
    }
    for name in ORDER:
        stages[name]() if name in stages else totals[name[0]].advance()
    frames_part = jnp.concatenate([v["frames", 0], v["frames", 1]], 0)
    frames_got = swaps.over_core(frames_part)
    output = jnp.concatenate(output, 0)
    output_got = swaps.over_core(output)
    packed = v["packed"]
    pieces = []
    start = 0
    for width in [model_width] * 7 + [units_here] + [local_width] * 2:
        pieces.append(packed[0, start : start + width])
        start += width
    (
        mask_embedding_grad,
        out_bias_grad,
        norm1_gain_grad,
        norm1_shift_grad,
        down_bias_grad,
        norm2_gain_grad,
        norm2_shift_grad,
        up_bias_grad,
        query_bias_grad,
        value_bias_grad,
    ) = pieces
    down_weight_grad, up_weight_grad, attn_weight_grad = (totals[name].finish() for name in "DUT")
    query_weight_grad, key_weight_grad, value_weight_grad, out_weight_grad = (
        attn_weight_grad[part * local_width : (part + 1) * local_width] for part in range(4)
    )
    query_weight_grad, key_weight_grad = query_weight_grad.T, key_weight_grad.T
    value_weight_grad = value_weight_grad.T

    def in_place(own, got):
        whole = jnp.stack([jnp.where(core == 0, own, got), jnp.where(core == 0, got, own)])
        return whole.reshape(token_rows, model_width)

    frames_grad = in_place(frames_part, frames_got) * (
        1.0 - frame_mask.reshape(token_rows, 1).astype(jnp.float32)
    )
    output = in_place(output, output_got) * norm2_gain + norm2_shift
    return (
        output.astype(jnp.bfloat16).reshape(frames.shape),
        frames_grad.astype(jnp.bfloat16).reshape(frames.shape),
        mask_embedding_grad,
        query_weight_grad,
        query_bias_grad,
        key_weight_grad,
        value_weight_grad,
        value_bias_grad,
        out_weight_grad,
        out_bias_grad,
        norm1_gain_grad,
        norm1_shift_grad,
        up_weight_grad,
        up_bias_grad,
        down_weight_grad,
        down_bias_grad,
        norm2_gain_grad,
        norm2_shift_grad,
    )


def solution(mesh):
    rows, columns, whole, vector = P("dp"), P(None, "tensor"), P(), P("tensor")
    return jax.shard_map(
        lambda *arrays: shards(mesh, *arrays),
        mesh=mesh,
        in_specs=(
            P("dp", None, None),
            P("dp", None),
            whole,
            columns,
            vector,
            columns,
            columns,
            vector,
            P("tensor", None),
            whole,
            whole,
            whole,
            columns,
            vector,
            P("tensor", None),
            whole,
            whole,
            whole,
            P("dp", None, None),
        ),
        out_specs=(
            P("dp", None, None),
            P("dp", None, None),
            whole,
            columns,
            vector,
            columns,
            columns,
            vector,
            P("tensor", None),
            whole,
            whole,
            whole,
            columns,
            vector,
            P("tensor", None),
            whole,
            whole,
            whole,
        ),
        check_vma=False,
    )
```

profile of v0, /device:TPU:0, one launch (start us, length us, event | category | flops | bytes accessed | tf_op | source)
XLA Modules:
  0.0 323.3 jit_solution(5414847180196594062)
XLA Ops:
  7.2 2.9 convert_multiply_fusion.1
  13.2 3.1 fusion.15
  19.1 1.9 multiply_reduce_fusion
  21.7 2.1 fusion
  23.8 3.5 %fusion.22 = bf16[3,64,1024]{2,1,0:T(8,128)(2,1)} fusion(bf16[1024,3,64]{0,2,1:T(8,128)(2,1)S(1)} %bitcast.149, f32[3,1024,1024]{1,2,0:T(8,128)S(1)} %get-tuple-element.378, f32[3,1024]{1,0:T(4,128)S(1)} %fusion, f32[3,1024]{1,0:T(4,128)S(1)} %get-tuple-element.377), kind=kOutput, calls=%fused_computation.58 | convolution fusion | flops 415432704 | bytes 13393920 | tf_op jit(solution)/shard_map/chqk,ckhd->cqhd/dot_general | solution.py:384
  31.7 2.8 collective-permute-start.1
  37.0 5.8 %all-gather.2.cloned.1.call-done.out_all = f32[768,768]{1,0:T(8,128)} async-done(((f32[192,768]{1,0:T(8,128)}), f32[768,768]{1,0:T(8,128)}) %all-gather.2.cloned.1.call-update) | async-done | bytes 2359312 | tf_op jit(solution)/shard_map/all_gather | solution.py:350
  48.7 2.2 shard_map.324
  51.0 1.8 fusion.30
  55.8 3.5 %fusion.8 = (f32[256,1536]{1,0:T(8,128)}, bf16[256,1536]{1,0:T(8,128)(2,1)S(1)}) fusion(f32[1536]{0:T(1024)S(1)} %reduce.6, bf16[256,768]{1,0:T(8,128)(2,1)} %get-tuple-element.301, bf16[768,1536]{1,0:T(8,128)(2,1)S(1)} %get-tuple-element.161.up), kind=kOutput, calls=%fused_computation.24 | convolution fusion | flops 608305152 | bytes 5117952 | tf_op jit(solution)/shard_map/dot_general | solution.py:22
  64.6 2.3 fusion.12
  66.9 1.7 fusion.53.part
  68.6 1.9 collective-permute-start.7
  70.6 2.0 dynamic-slice_bitcast_fusion
  72.6 2.2 copy.42
  74.9 2.2 copy.43
  81.7 5.4 %shard_map.325 = (f32[256,768]{1,0:T(8,128)S(1)}, f32[256,768]{1,0:T(8,128)S(1)}, bf16[256,768]{1,0:T(8,128)(2,1)S(1)}, bf16[256,1536]{1,0:T(8,128)(2,1)S(1)}, f...) custom-call(f32[256,768]{1,0:T(8,128)S(1)} %copy-done.6, f32[256,768]{1,0:T(8,128)} %fusion.52.part, ...), custom_call_target="tpu_custom_call" | custom-call | flops 1 | bytes 1 | tf_op jit(solution)/shard_map/pallas_call | solution.py:181
  88.1 10.4 %collective-permute-done.7.got = f32[256,768]{1,0:T(8,128)} collective-permute-done((f32[256,768]{1,0:T(8,128)}, f32[256,768]{1,0:T(8,128)}, u32[]{:S(2)}, u32[]{:S(2)}) %collective-permute-start.7) | collective-permute-done | bytes 786464 | tf_op jit(solution)/shard_map/ppermute | solution.py:66
  98.5 5.5 %shard_map.326 = (f32[256,768]{1,0:T(8,128)S(1)}, f32[256,768]{1,0:T(8,128)S(1)}, bf16[256,768]{1,0:T(8,128)(2,1)S(1)}, bf16[256,1536]{1,0:T(8,128)(2,1)S(1)}, f...) custom-call(f32[256,768]{1,0:T(8,128)S(1)} %copy-done.7, f32[256,768]{1,0:T(8,128)} %fusion.53.part, ...), custom_call_target="tpu_custom_call" | custom-call | flops 1 | bytes 1 | tf_op jit(solution)/shard_map/pallas_call | solution.py:181
  104.1 2.2 fusion.54
  106.4 2.3 fusion.55
  108.9 2.2 fusion.56
  111.1 3.4 %collective-permute-done.9.got = f32[256,768]{1,0:T(8,128)S(1)} collective-permute-done((f32[256,768]{1,0:T(8,128)S(1)}, f32[256,768]{1,0:T(8,128)S(1)}, u32[]{:S(2)}, u32[]{:S(2)}) %collective-permute-start.9) | collective-permute-done | bytes 786464 | tf_op jit(solution)/shard_map/ppermute | solution.py:66
  115.6 2.2 fusion.57
  118.0 4.3 %dynamic-slice_add_fusion.2 = (f32[384,768]{1,0:T(8,128)}, f32[384,768]{1,0:T(8,128)}) fusion(f32[768,768]{1,0:T(8,128)} %collective-permute-done.12, s32[]{:T(128)S(6)} %select_n.140, f32[768,768]{1,0:T(8,128)} %fusion.54, s32[]{:T(128)S(6)} %select_n.139), kind=kLoop, calls=%fused_computation.65 | loop fusion | flops 589824 | bytes 7077896 | tf_op jit(solution)/shard_map/add | solution.py:142
  123.7 3.4 %dynamic-slice_add_fusion = (f32[384,768]{1,0:T(8,128)}, f32[384,768]{1,0:T(8,128)}) fusion(f32[768,768]{1,0:T(8,128)} %collective-permute-done.11, s32[]{:T(128)S(6)} %select_n.140, f32[768,768]{1,0:T(8,128)S(1)} %copy-done.52, s32[]{:T(128)S(6)} %select_n.139), kind=kLoop, calls=%fused_computation.63 | loop fusion | flops 589824 | bytes 7077896 | tf_op jit(solution)/shard_map/add | solution.py:142
  132.4 10.7 %collective-permute-done.10.got = f32[256,768]{1,0:T(8,128)} collective-permute-done((f32[256,768]{1,0:T(8,128)S(1)}, f32[256,768]{1,0:T(8,128)}, u32[]{:S(2)}, u32[]{:S(2)}) %collective-permute-start.10) | collective-permute-done | bytes 786464 | tf_op jit(solution)/shard_map/ppermute | solution.py:66
  143.1 2.3 shard_map.328
  148.2 2.5 dynamic-slice_add_fusion.8
  153.1 2.5 dynamic-slice_add_fusion.6
  159.1 10.5 %shard_map.329 = (bf16[3,64,1024]{2,1,0:T(8,128)(2,1)S(1)}, bf16[3,1024,64]{2,1,0:T(8,128)(2,1)S(1)}, bf16[3,1024,64]{2,1,0:T(8,128)(2,1)S(1)}) custom-call(bf16[3,1024,64]{2,1,0:T(8,128)(2,1)S(1)} %bitcast.136, bf16[3,1024,64]{2,1,0:T(8,128)(2,1)S(1)} %copy-done.11, bf16[3,1024,64]{2,1,0:T(8,128)(2,1)S(1)} %bitcast.137, f32[3,1,1024]{2,1,0:T(1,128)S(1)} %add.341.sums, ...), custom_call_target="tpu_custom_call" | custom-call | flops 1 | bytes 1 | tf_op jit(solution)/shard_map/pallas_call | solution.py:181
  177.1 2.1 select_bitcast_fusion.3
  182.0 2.1 collective-permute-start.22
  189.0 16.9 %collective-permute-done.19 = f32[192,768]{1,0:T(8,128)S(1)} collective-permute-done((f32[192,768]{1,0:T(8,128)S(1)}, f32[192,768]{1,0:T(8,128)S(1)}, u32[]{:S(2)}, u32[]{:S(2)}) %collective-permute-start.19) | collective-permute-done | bytes 589856 | tf_op jit(solution)/shard_map/ppermute | solution.py:66
  207.1 2.8 collective-permute-done.22
  210.8 2.3 collective-permute-start.23
  215.5 2.3 collective-permute-start.28
  217.7 1.7 dynamic-slice_add_fusion.4
  219.6 11.5 %collective-permute-done.23 = f32[192,768]{1,0:T(8,128)} collective-permute-done((f32[192,768]{1,0:T(8,128)}, f32[192,768]{1,0:T(8,128)}, u32[]{:S(2)}, u32[]{:S(2)}) %collective-permute-start.23) | collective-permute-done | bytes 589856 | tf_op jit(solution)/shard_map/ppermute | solution.py:66
  236.9 5.8 %collective-permute-done.28 = f32[192,768]{1,0:T(8,128)S(1)} collective-permute-done((f32[192,768]{1,0:T(8,128)}, f32[192,768]{1,0:T(8,128)S(1)}, u32[]{:S(2)}, u32[]{:S(2)}) %collective-permute-start.28) | collective-permute-done | bytes 589856 | tf_op jit(solution)/shard_map/ppermute | solution.py:66
  243.0 12.5 %collective-permute-done.27 = f32[192,768]{1,0:T(8,128)S(1)} collective-permute-done((f32[192,768]{1,0:T(8,128)S(1)}, f32[192,768]{1,0:T(8,128)S(1)}, u32[]{:S(2)}, u32[]{:S(2)}) %collective-permute-start.27) | collective-permute-done | bytes 589856 | tf_op jit(solution)/shard_map/ppermute | solution.py:66
  258.5 15.3 %collective-permute-done.31 = f32[192,768]{1,0:T(8,128)} collective-permute-done((f32[192,768]{1,0:T(8,128)S(1)}, f32[192,768]{1,0:T(8,128)}, u32[]{:S(2)}, u32[]{:S(2)}) %collective-permute-start.31) | collective-permute-done | bytes 589856 | tf_op jit(solution)/shard_map/ppermute | solution.py:66
  275.4 2.3 collective-permute-done.30
  278.8 3.0 collective-permute-start.36
  282.0 1.8 broadcast_select_fusion.5
  285.3 7.6 %collective-permute-done.32 = f32[1,6528]{1,0:T(1,128)S(1)} collective-permute-done((f32[1,6528]{1,0:T(1,128)S(1)}, f32[1,6528]{1,0:T(1,128)S(1)}, u32[]{:S(2)}, u32[]{:S(2)}) %collective-permute-start.32) | collective-permute-done | bytes 26144 | tf_op jit(solution)/shard_map/ppermute | solution.py:66
  293.0 2.4 collective-permute-start.34
  302.4 11.3 %collective-permute-done.37 = f32[384,768]{1,0:T(8,128)S(1)} collective-permute-done((f32[384,768]{1,0:T(8,128)S(1)}, f32[384,768]{1,0:T(8,128)S(1)}, u32[]{:S(2)}, u32[]{:S(2)}) %collective-permute-start.37) | collective-permute-done | bytes 1179680 | tf_op jit(solution)/shard_map/ppermute | solution.py:66
  (368 shorter events, 91.5 us)
Async XLA Ops:
  7.2 35.6 %all-gather.2.cloned.1.call-start = ((), (), s32[]{:S(2)}) async-start(), calls=%async_computation | async-start | bytes 2949120 | tf_op jit(solution)/shard_map/all_gather | solution.py:350
  10.2 25.5 %collective-permute-start.2 = (f32[768,768]{1,0:T(8,128)}, f32[768,768]{1,0:T(8,128)}, u32[]{:S(2)}, u32[]{:S(2)}) collective-permute-start(f32[768,768]{1,0:T(8,128)} %convert_multiply_fusion.1), channel_id=1, source_target_pairs={{0,1},{1,0},{2,3},{3,2},{4,5},{5,4},{6,7},{7,6},{8,9},{9,8},{10,11... | collective-permute-start | bytes 7077896 | tf_op jit(solution)/shard_map/ppermute | solution.py:66
  12.2 23.4 %collective-permute-start.3 = (f32[768,768]{1,0:T(8,128)}, f32[768,768]{1,0:T(8,128)S(1)}, u32[]{:S(2)}, u32[]{:S(2)}) collective-permute-start(f32[768,768]{1,0:T(8,128)} %convert_multiply_fusion), channel_id=1, source_target_pairs={{0,1},{1,0},{2,3},{3,2},{4,5},{5,4},{6,7},{7,6},{8,9},{9,8},{10,11... | collective-permute-start | bytes 7077896 | tf_op jit(solution)/shard_map/ppermute | solution.py:66
  28.6 2.1 collective-permute-start
  31.7 19.3 %collective-permute-start.1 = (f32[256,384]{1,0:T(8,128)}, f32[256,384]{1,0:T(8,128)}, u32[]{:S(2)}, u32[]{:S(2)}) collective-permute-start(f32[256,384]{1,0:T(8,128)} %get-tuple-element.154), channel_id=1, source_target_pairs={{0,2},{1,3},{2,0},{3,1},{4,6},{5,7},{6,4},{7,5},{8,10},{9,11},{10,... | collective-permute-start | bytes 1179656 | tf_op jit(solution)/shard_map/ppermute | solution.py:66
  34.6 8.3 %collective-permute-start.4 = (f32[1,768]{1,0:T(1,128)S(1)}, f32[1,768]{1,0:T(1,128)S(1)}, u32[]{:S(2)}, u32[]{:S(2)}) collective-permute-start(f32[1,768]{1,0:T(1,128)S(1)} %reshape.385.bias), channel_id=1, source_target_pairs={{0,1},{1,0},{2,3},{3,2},{4,5},{5,4},{6,7},{7,6},{8,9},{9,8},{10,11... | collective-permute-start | bytes 9224 | tf_op jit(solution)/shard_map/ppermute | solution.py:66
  35.4 25.5 %collective-permute-start.6 = (f32[256,384]{1,0:T(8,128)}, f32[256,384]{1,0:T(8,128)}, u32[]{:S(2)}, u32[]{:S(2)}) collective-permute-start(f32[256,384]{1,0:T(8,128)} %get-tuple-element.155), channel_id=1, source_target_pairs={{0,2},{1,3},{2,0},{3,1},{4,6},{5,7},{6,4},{7,5},{8,10},{9,11},{10,... | collective-permute-start | bytes 1179656 | tf_op jit(solution)/shard_map/ppermute | solution.py:66
  60.9 20.7 %collective-permute-start.5 = (f32[256,768]{1,0:T(8,128)}, f32[256,768]{1,0:T(8,128)}, u32[]{:S(2)}, u32[]{:S(2)}) collective-permute-start(f32[256,768]{1,0:T(8,128)} %fusion.52.part), channel_id=1, source_target_pairs={{0,2},{1,3},{2,0},{3,1},{4,6},{5,7},{6,4},{7,5},{8,10},{9,11},{10,... | collective-permute-start | bytes 2359304 | tf_op jit(solution)/shard_map/ppermute | solution.py:66
  68.6 29.9 %collective-permute-start.7 = (f32[256,768]{1,0:T(8,128)}, f32[256,768]{1,0:T(8,128)}, u32[]{:S(2)}, u32[]{:S(2)}) collective-permute-start(f32[256,768]{1,0:T(8,128)} %fusion.53.part), channel_id=1, source_target_pairs={{0,2},{1,3},{2,0},{3,1},{4,6},{5,7},{6,4},{7,5},{8,10},{9,11},{10,... | collective-permute-start | bytes 2359304 | tf_op jit(solution)/shard_map/ppermute | solution.py:66
  80.2 34.4 %copy-start.14 = (bf16[192,768]{1,0:T(8,128)(2,1)}, bf16[192,768]{1,0:T(8,128)(2,1)S(1)}, u32[]{:S(2)}) copy-start(bf16[192,768]{1,0:T(8,128)(2,1)S(1)} %get-tuple-element.353.pair) | copy-start | bytes 884740
  80.2 34.4 %copy-start.16 = (bf16[192,768]{1,0:T(8,128)(2,1)}, bf16[192,768]{1,0:T(8,128)(2,1)S(1)}, u32[]{:S(2)}) copy-start(bf16[192,768]{1,0:T(8,128)(2,1)S(1)} %get-tuple-element.354.own) | copy-start | bytes 884740
  81.7 16.9 %copy-start.7 = (f32[256,768]{1,0:T(8,128)S(1)}, f32[256,768]{1,0:T(8,128)}, u32[]{:S(2)}) copy-start(f32[256,768]{1,0:T(8,128)} %get-tuple-element.299.hidden) | copy-start | bytes 2359300
  81.7 16.9 %copy-start.25 = (bf16[256,768]{1,0:T(8,128)(2,1)S(1)}, bf16[256,768]{1,0:T(8,128)(2,1)}, u32[]{:S(2)}) copy-start(bf16[256,768]{1,0:T(8,128)(2,1)} %get-tuple-element.339.cotangent) | copy-start | bytes 1179652
  81.7 16.9 %copy-start.28 = (f32[256,1536]{1,0:T(8,128)S(1)}, f32[256,1536]{1,0:T(8,128)}, u32[]{:S(2)}) copy-start(f32[256,1536]{1,0:T(8,128)} %get-tuple-element.337.slope) | copy-start | bytes 4718596
  88.1 26.5 %collective-permute-start.9 = (f32[256,768]{1,0:T(8,128)S(1)}, f32[256,768]{1,0:T(8,128)S(1)}, u32[]{:S(2)}, u32[]{:S(2)}) collective-permute-start(f32[256,768]{1,0:T(8,128)S(1)} %get-tuple-element.190.part), channel_id=1, source_target_pairs={{0,2},{1,3},{2,0},{3,1},{4,6},{5,7},{6,4},{7,5},{8,10},{9,11},{10,... | collective-permute-start | bytes 2359304 | tf_op jit(solution)/shard_map/ppermute | solution.py:66
  108.7 9.3 %collective-permute-start.12 = (f32[768,768]{1,0:T(8,128)}, f32[768,768]{1,0:T(8,128)}, u32[]{:S(2)}, u32[]{:S(2)}) collective-permute-start(f32[768,768]{1,0:T(8,128)} %fusion.55), channel_id=1, source_target_pairs={{0,1},{1,0},{2,3},{3,2},{4,5},{5,4},{6,7},{7,6},{8,9},{9,8},{10,11... | collective-permute-start | bytes 7077896 | tf_op jit(solution)/shard_map/ppermute | solution.py:66
  117.9 5.8 %collective-permute-start.11 = (f32[768,768]{1,0:T(8,128)}, f32[768,768]{1,0:T(8,128)}, u32[]{:S(2)}, u32[]{:S(2)}) collective-permute-start(f32[768,768]{1,0:T(8,128)} %fusion.57), channel_id=1, source_target_pairs={{0,1},{1,0},{2,3},{3,2},{4,5},{5,4},{6,7},{7,6},{8,9},{9,8},{10,11... | collective-permute-start | bytes 7077896 | tf_op jit(solution)/shard_map/ppermute | solution.py:66
  122.3 25.8 %collective-permute-start.15 = (f32[384,768]{1,0:T(8,128)}, f32[384,768]{1,0:T(8,128)}, u32[]{:S(2)}, u32[]{:S(2)}) collective-permute-start(f32[384,768]{1,0:T(8,128)} %get-tuple-element.307), channel_id=1, source_target_pairs={{0,4},{1,9},{2,6},{3,11},{4,0},{5,13},{6,2},{7,15},{8,12},{9,1},{1... | collective-permute-start | bytes 3538952 | tf_op jit(solution)/shard_map/ppermute | solution.py:66
  123.4 19.7 %collective-permute-start.10 = (f32[256,768]{1,0:T(8,128)S(1)}, f32[256,768]{1,0:T(8,128)}, u32[]{:S(2)}, u32[]{:S(2)}) collective-permute-start(f32[256,768]{1,0:T(8,128)S(1)} %copy-done.41), channel_id=1, source_target_pairs={{0,2},{1,3},{2,0},{3,1},{4,6},{5,7},{6,4},{7,5},{8,10},{9,11},{10,... | collective-permute-start | bytes 2359304 | tf_op jit(solution)/shard_map/ppermute | solution.py:66
  123.7 19.4 %copy-start.39 = (f32[256,768]{1,0:T(8,128)S(1)}, f32[256,768]{1,0:T(8,128)}, u32[]{:S(2)}) copy-start(f32[256,768]{1,0:T(8,128)} %copy-done.38) | copy-start | bytes 2359300
  127.1 16.0 %copy-start.17 = (bf16[192,768]{1,0:T(8,128)(2,1)S(1)}, bf16[192,768]{1,0:T(8,128)(2,1)}, u32[]{:S(2)}) copy-start(bf16[192,768]{1,0:T(8,128)(2,1)} %copy-done.16) | copy-start | bytes 884740
  127.1 26.0 %collective-permute-start.14 = (f32[384,768]{1,0:T(8,128)}, f32[384,768]{1,0:T(8,128)}, u32[]{:S(2)}, u32[]{:S(2)}) collective-permute-start(f32[384,768]{1,0:T(8,128)} %get-tuple-element.305), channel_id=1, source_target_pairs={{0,4},{1,9},{2,6},{3,11},{4,0},{5,13},{6,2},{7,15},{8,12},{9,1},{1... | collective-permute-start | bytes 3538952 | tf_op jit(solution)/shard_map/ppermute | solution.py:66
  145.5 6.0 %collective-permute-start.13 = (f32[512,192]{1,0:T(8,128)S(1)}, f32[512,192]{1,0:T(8,128)S(1)}, u32[]{:S(2)}, u32[]{:S(2)}) collective-permute-start(f32[512,192]{1,0:T(8,128)S(1)} %pad_maximum_fusion.13), channel_id=1, source_target_pairs={{0,1},{1,0},{2,3},{3,2},{4,5},{5,4},{6,7},{7,6},{8,9},{9,8},{10,11... | collective-permute-start | bytes 1179656 | tf_op jit(solution)/shard_map/ppermute | solution.py:66
  148.1 29.0 %collective-permute-start.8 = (f32[512,768]{1,0:T(8,128)}, f32[512,768]{1,0:T(8,128)}, u32[]{:S(2)}, u32[]{:S(2)}) collective-permute-start(f32[512,768]{1,0:T(8,128)} %constant_dynamic-update-slice_fusion), channel_id=1, source_target_pairs={{0,1},{1,0},{2,3},{3,2},{4,5},{5,4},{6,7},{7,6},{8,9},{9,8},{10,11... | collective-permute-start | bytes 4718600 | tf_op jit(solution)/shard_map/ppermute | solution.py:66
  150.6 23.2 %collective-permute-start.16 = (f32[192,768]{1,0:T(8,128)}, f32[192,768]{1,0:T(8,128)}, u32[]{:S(2)}, u32[]{:S(2)}) collective-permute-start(f32[192,768]{1,0:T(8,128)} %get-tuple-element.325), channel_id=1, source_target_pairs={{0,8},{1,5},{2,10},{3,7},{4,12},{5,1},{6,14},{7,3},{8,0},{9,13},{1... | collective-permute-start | bytes 1769480 | tf_op jit(solution)/shard_map/ppermute | solution.py:66
  176.1 3.8 %collective-permute-start.17 = (f32[512,768]{1,0:T(8,128)S(1)}, f32[512,768]{1,0:T(8,128)S(1)}, u32[]{:S(2)}, u32[]{:S(2)}) collective-permute-start(f32[512,768]{1,0:T(8,128)S(1)} %fusion.24), channel_id=1, source_target_pairs={{0,1},{1,0},{2,3},{3,2},{4,5},{5,4},{6,7},{7,6},{8,9},{9,8},{10,11... | collective-permute-start | bytes 4718600 | tf_op jit(solution)/shard_map/ppermute | solution.py:66
  180.5 5.0 %collective-permute-start.20 = (f32[192,768]{1,0:T(8,128)S(1)}, f32[192,768]{1,0:T(8,128)S(1)}, u32[]{:S(2)}, u32[]{:S(2)}) collective-permute-start(f32[192,768]{1,0:T(8,128)S(1)} %fusion.58), channel_id=1, source_target_pairs={{0,1},{1,0},{2,3},{3,2},{4,5},{5,4},{6,7},{7,6},{8,9},{9,8},{10,11... | collective-permute-start | bytes 1769480 | tf_op jit(solution)/shard_map/ppermute | solution.py:66
  181.3 24.7 %collective-permute-start.19 = (f32[192,768]{1,0:T(8,128)S(1)}, f32[192,768]{1,0:T(8,128)S(1)}, u32[]{:S(2)}, u32[]{:S(2)}) collective-permute-start(f32[192,768]{1,0:T(8,128)S(1)} %copy-done.69), channel_id=1, source_target_pairs={{0,8},{1,5},{2,10},{3,7},{4,12},{5,1},{6,14},{7,3},{8,0},{9,13},{1... | collective-permute-start | bytes 1769480 | tf_op jit(solution)/shard_map/ppermute | solution.py:66
  182.0 27.9 %collective-permute-start.22 = (f32[192,768]{1,0:T(8,128)S(1)}, f32[192,768]{1,0:T(8,128)S(1)}, u32[]{:S(2)}, u32[]{:S(2)}) collective-permute-start(f32[192,768]{1,0:T(8,128)S(1)} %add.358), channel_id=1, source_target_pairs={{0,16},{1,17},{2,18},{3,19},{4,20},{5,21},{6,22},{7,23},{8,24},{9,... | collective-permute-start | bytes 1769480 | tf_op jit(solution)/shard_map/ppermute | solution.py:66
  184.1 22.7 %collective-permute-start.18 = (f32[256,768]{1,0:T(8,128)S(1)}, f32[256,768]{1,0:T(8,128)S(1)}, u32[]{:S(2)}, u32[]{:S(2)}) collective-permute-start(f32[256,768]{1,0:T(8,128)S(1)} %add.359), channel_id=1, source_target_pairs={{0,2},{1,3},{2,0},{3,1},{4,6},{5,7},{6,4},{7,5},{8,10},{9,11},{10,... | collective-permute-start | bytes 2359304 | tf_op jit(solution)/shard_map/ppermute | solution.py:66
  187.3 30.4 %collective-permute-start.24 = (f32[384,768]{1,0:T(8,128)}, f32[384,768]{1,0:T(8,128)}, u32[]{:S(2)}, u32[]{:S(2)}) collective-permute-start(f32[384,768]{1,0:T(8,128)} %get-tuple-element.321), channel_id=1, source_target_pairs={{0,4},{1,9},{2,6},{3,11},{4,0},{5,13},{6,2},{7,15},{8,12},{9,1},{1... | collective-permute-start | bytes 3538952 | tf_op jit(solution)/shard_map/ppermute | solution.py:66
  188.8 17.2 %copy-start.59 = (f32[192,768]{1,0:T(8,128)S(1)}, f32[192,768]{1,0:T(8,128)}, u32[]{:S(2)}) copy-start(f32[192,768]{1,0:T(8,128)} %get-tuple-element.235) | copy-start | bytes 1769476
  189.0 17.9 %copy-start.35 = (f32[256,768]{1,0:T(8,128)S(1)}, f32[256,768]{1,0:T(8,128)}, u32[]{:S(2)}) copy-start(f32[256,768]{1,0:T(8,128)} %copy-done.34) | copy-start | bytes 2359300
  210.8 20.3 %collective-permute-start.23 = (f32[192,768]{1,0:T(8,128)}, f32[192,768]{1,0:T(8,128)}, u32[]{:S(2)}, u32[]{:S(2)}) collective-permute-start(f32[192,768]{1,0:T(8,128)} %add.365), channel_id=1, source_target_pairs={{0,8},{1,5},{2,10},{3,7},{4,12},{5,1},{6,14},{7,3},{8,0},{9,13},{1... | collective-permute-start | bytes 1769480 | tf_op jit(solution)/shard_map/ppermute | solution.py:66
  214.6 19.7 %collective-permute-start.21 = (f32[256,768]{1,0:T(8,128)S(1)}, f32[256,768]{1,0:T(8,128)}, u32[]{:S(2)}, u32[]{:S(2)}) collective-permute-start(f32[256,768]{1,0:T(8,128)S(1)} %add.360), channel_id=1, source_target_pairs={{0,2},{1,3},{2,0},{3,1},{4,6},{5,7},{6,4},{7,5},{8,10},{9,11},{10,... | collective-permute-start | bytes 2359304 | tf_op jit(solution)/shard_map/ppermute | solution.py:66
  215.5 27.2 %collective-permute-start.28 = (f32[192,768]{1,0:T(8,128)}, f32[192,768]{1,0:T(8,128)S(1)}, u32[]{:S(2)}, u32[]{:S(2)}) collective-permute-start(f32[192,768]{1,0:T(8,128)} %add.362), channel_id=1, source_target_pairs={{0,16},{1,17},{2,18},{3,19},{4,20},{5,21},{6,22},{7,23},{8,24},{9,... | collective-permute-start | bytes 1769480 | tf_op jit(solution)/shard_map/ppermute | solution.py:66
  219.5 36.0 %collective-permute-start.27 = (f32[192,768]{1,0:T(8,128)S(1)}, f32[192,768]{1,0:T(8,128)S(1)}, u32[]{:S(2)}, u32[]{:S(2)}) collective-permute-start(f32[192,768]{1,0:T(8,128)S(1)} %get-tuple-element.319), channel_id=1, source_target_pairs={{0,8},{1,5},{2,10},{3,7},{4,12},{5,1},{6,14},{7,3},{8,0},{9,13},{1... | collective-permute-start | bytes 1769480 | tf_op jit(solution)/shard_map/ppermute | solution.py:66
  233.5 48.4 %collective-permute-start.33 = (f32[384,768]{1,0:T(8,128)}, f32[384,768]{1,0:T(8,128)}, u32[]{:S(2)}, u32[]{:S(2)}) collective-permute-start(f32[384,768]{1,0:T(8,128)} %pad_maximum_fusion.8), channel_id=1, source_target_pairs={{0,4},{1,9},{2,6},{3,11},{4,0},{5,13},{6,2},{7,15},{8,12},{9,1},{1... | collective-permute-start | bytes 3538952 | tf_op jit(solution)/shard_map/ppermute | solution.py:66
  242.7 31.0 %collective-permute-start.31 = (f32[192,768]{1,0:T(8,128)S(1)}, f32[192,768]{1,0:T(8,128)}, u32[]{:S(2)}, u32[]{:S(2)}) collective-permute-start(f32[192,768]{1,0:T(8,128)S(1)} %add.384), channel_id=1, source_target_pairs={{0,8},{1,5},{2,10},{3,7},{4,12},{5,1},{6,14},{7,3},{8,0},{9,13},{1... | collective-permute-start | bytes 1769480 | tf_op jit(solution)/shard_map/ppermute | solution.py:66
  242.8 52.6 %collective-permute-start.25 = (f32[512,768]{1,0:T(8,128)}, f32[512,768]{1,0:T(8,128)}, u32[]{:S(2)}, u32[]{:S(2)}) collective-permute-start(f32[512,768]{1,0:T(8,128)} %pad_maximum_fusion.6), channel_id=1, source_target_pairs={{0,1},{1,0},{2,3},{3,2},{4,5},{5,4},{6,7},{7,6},{8,9},{9,8},{10,11... | collective-permute-start | bytes 4718600 | tf_op jit(solution)/shard_map/ppermute | solution.py:66
  255.6 22.1 %collective-permute-start.30 = (f32[192,768]{1,0:T(8,128)S(1)}, f32[192,768]{1,0:T(8,128)}, u32[]{:S(2)}, u32[]{:S(2)}) collective-permute-start(f32[192,768]{1,0:T(8,128)S(1)} %add.385), channel_id=1, source_target_pairs={{0,16},{1,17},{2,18},{3,19},{4,20},{5,21},{6,22},{7,23},{8,24},{9,... | collective-permute-start | bytes 1769480 | tf_op jit(solution)/shard_map/ppermute | solution.py:66
  255.6 1.3 collective-permute-start.26
  257.0 24.8 %collective-permute-start.29 = (f32[1,6528]{1,0:T(1,128)S(1)}, f32[1,6528]{1,0:T(1,128)S(1)}, u32[]{:S(2)}, u32[]{:S(2)}) collective-permute-start(f32[1,6528]{1,0:T(1,128)S(1)} %concatenate.79), channel_id=1, source_target_pairs={{0,4},{1,5},{2,6},{3,7},{4,0},{5,1},{6,2},{7,3},{8,12},{9,13},{10,... | collective-permute-start | bytes 78344 | tf_op jit(solution)/shard_map/ppermute | solution.py:66
  275.0 24.3 %collective-permute-start.35 = (f32[384,768]{1,0:T(8,128)S(1)}, f32[384,768]{1,0:T(8,128)S(1)}, u32[]{:S(2)}, u32[]{:S(2)}) collective-permute-start(f32[384,768]{1,0:T(8,128)S(1)} %pad_maximum_fusion.9), channel_id=1, source_target_pairs={{0,4},{1,9},{2,6},{3,11},{4,0},{5,13},{6,2},{7,15},{8,12},{9,1},{1... | collective-permute-start | bytes 3538952 | tf_op jit(solution)/shard_map/ppermute | solution.py:66
  278.8 18.4 %collective-permute-start.36 = (f32[192,768]{1,0:T(8,128)S(1)}, f32[192,768]{1,0:T(8,128)S(1)}, u32[]{:S(2)}, u32[]{:S(2)}) collective-permute-start(f32[192,768]{1,0:T(8,128)S(1)} %add.387), channel_id=1, source_target_pairs={{0,8},{1,5},{2,10},{3,7},{4,12},{5,1},{6,14},{7,3},{8,0},{9,13},{1... | collective-permute-start | bytes 1769480 | tf_op jit(solution)/shard_map/ppermute | solution.py:66
  281.9 11.1 %collective-permute-start.32 = (f32[1,6528]{1,0:T(1,128)S(1)}, f32[1,6528]{1,0:T(1,128)S(1)}, u32[]{:S(2)}, u32[]{:S(2)}) collective-permute-start(f32[1,6528]{1,0:T(1,128)S(1)} %add.388), channel_id=1, source_target_pairs={{0,8},{1,9},{2,10},{3,11},{4,12},{5,13},{6,14},{7,15},{8,0},{9,1},... | collective-permute-start | bytes 78344 | tf_op jit(solution)/shard_map/ppermute | solution.py:66
  293.0 8.0 %collective-permute-start.34 = (f32[1,6528]{1,0:T(1,128)S(1)}, f32[1,6528]{1,0:T(1,128)S(1)}, u32[]{:S(2)}, u32[]{:S(2)}) collective-permute-start(f32[1,6528]{1,0:T(1,128)S(1)} %add.389), channel_id=1, source_target_pairs={{0,16},{1,17},{2,18},{3,19},{4,20},{5,21},{6,22},{7,23},{8,24},{9,... | collective-permute-start | bytes 78344 | tf_op jit(solution)/shard_map/ppermute | solution.py:66
  297.4 16.3 %collective-permute-start.37 = (f32[384,768]{1,0:T(8,128)S(1)}, f32[384,768]{1,0:T(8,128)S(1)}, u32[]{:S(2)}, u32[]{:S(2)}) collective-permute-start(f32[384,768]{1,0:T(8,128)S(1)} %pad_maximum_fusion.10), channel_id=1, source_target_pairs={{0,4},{1,9},{2,6},{3,11},{4,0},{5,13},{6,2},{7,15},{8,12},{9,1},{1... | collective-permute-start | bytes 3538952 | tf_op jit(solution)/shard_map/ppermute | solution.py:66
  (83 other events, 263.7 us)
Sparse Core Ops, SparseCore 0:
  13.2 29.5 all-gather.1
where the time goes:
time: 329 us; the launch traced here: 323 us
  waiting for transfers between devices  121 us (37%)
  other arithmetic  55.4 us (17%)
  local copies, waits for them, and re-layouts  40.4 us (12%)
  matrix products  33.1 us (10%)
  starting transfers between devices  29.2 us (9%)
  Pallas kernels  28.2 us (9%)
  between operations  16.1 us (5%)
    ppermute x38, waiting for transfers between devices, move(): return lax.ppermute(value, AXES, pairs)  115 us
    ppermute x38, starting transfers between devices, move(): return lax.ppermute(value, AXES, pairs)  29.2 us
    pallas_call x8, Pallas kernels, kernel_call(): pl.pallas_call(body, out_shape=shapes, cost_estimate=pl.CostEstimate(flop...  28.2 us
    unnamed x196, local copies, waits for them, and re-layouts  18.9 us
    dot_general x11, matrix products, local_dot(): return jnp.dot(left, right, preferred_element_type=jnp.float32)  15.4 us
    add x5, other arithmetic, halve(): self.keep = pick(keep, coord, rows) + pick(got, coord, rows)  14.4 us
    dot_general x7, matrix products, dot_rows(): lax.dot_general(left, right, (((0,), (0,)), ((), ())), preferred_element_...  10.7 us
  transfers between devices with their start and end apart: 39, of which 17 were waited for; matrix products, arithmetic and copies ran while one was open for 33% of the time, Pallas kernels for 9%

commit v1 on v0

--- a/solution.py
+++ b/solution.py
@@ -13,8 +13,8 @@
 TURNS = (True, True, True)
 ORDER = (
     "Dk", "Ds", "Uk", "N0", "Us", "D1", "U1", "N1", "D2", "U2", "at", "tk", "D3", "ts", "A0",
-    "A1", "os", "qk", "T1", "U3", "F0", "D4", "T2", "D5", "F1", "U4", "T3", "V", "U5", "T4",
-    "V0", "D6", "V1", "T5", "U6", "V2", "T6",
+    "A1", "os", "qk", "U3", "T1", "F0", "D4", "T2", "D5", "F1", "U4", "T3", "V", "U5", "V0",
+    "T4", "D6", "V1", "T5", "V2", "U6", "T6",
 )
 
 

time: 329 us -> 326 us (level)
  the two profiles are of different devices: /device:TPU:0 before, /device:TPU:1 now
where the time goes in v1:
time: 326 us; the launch traced here: 320 us
  waiting for transfers between devices  112 us (34%)
  other arithmetic  55.4 us (17%)
  local copies, waits for them, and re-layouts  40 us (12%)
  starting transfers between devices  35.1 us (11%)
  matrix products  33.1 us (10%)
  Pallas kernels  28.2 us (9%)
  between operations  15.9 us (5%)
    ppermute x38, waiting for transfers between devices, move(): return lax.ppermute(value, AXES, pairs)  106 us
    ppermute x38, starting transfers between devices, move(): return lax.ppermute(value, AXES, pairs)  35 us
    pallas_call x8, Pallas kernels, kernel_call(): pl.pallas_call(body, out_shape=shapes, cost_estimate=pl.CostEstimate(flop...  28.2 us
    unnamed x196, local copies, waits for them, and re-layouts  18.6 us
    dot_general x11, matrix products, local_dot(): return jnp.dot(left, right, preferred_element_type=jnp.float32)  15.4 us
    add x5, other arithmetic, halve(): self.keep = pick(keep, coord, rows) + pick(got, coord, rows)  14.4 us
    dot_general x7, matrix products, dot_rows(): lax.dot_general(left, right, (((0,), (0,)), ((), ())), preferred_element_...  10.7 us
  transfers between devices with their start and end apart: 39, of which 19 were waited for; matrix products, arithmetic and copies ran while one was open for 34% of the time, Pallas kernels for 9%

profile of v1, /device:TPU:1, one launch (start us, length us, event | category | flops | bytes accessed | tf_op | source)
XLA Modules:
  0.0 319.6 jit_solution(10020565053104290275)
XLA Ops:
  7.2 2.9 convert_multiply_fusion.1
  13.2 3.1 fusion.15
  19.1 1.9 multiply_reduce_fusion
  21.7 2.1 fusion
  23.8 3.5 %fusion.22 = bf16[3,64,1024]{2,1,0:T(8,128)(2,1)} fusion(bf16[1024,3,64]{0,2,1:T(8,128)(2,1)S(1)} %bitcast.149, f32[3,1024,1024]{1,2,0:T(8,128)S(1)} %get-tuple-element.378, f32[3,1024]{1,0:T(4,128)S(1)} %fusion, f32[3,1024]{1,0:T(4,128)S(1)} %get-tuple-element.377), kind=kOutput, calls=%fused_computation.58 | convolution fusion | flops 415432704 | bytes 13393920 | tf_op jit(solution)/shard_map/chqk,ckhd->cqhd/dot_general | solution.py:384
  28.7 1.9 collective-permute-done.pair
  31.7 2.3 collective-permute-start.1
  36.9 5.8 %all-gather.2.cloned.1.call-done.out_all = f32[768,768]{1,0:T(8,128)} async-done(((f32[192,768]{1,0:T(8,128)}), f32[768,768]{1,0:T(8,128)}) %all-gather.2.cloned.1.call-update) | async-done | bytes 2359312 | tf_op jit(solution)/shard_map/all_gather | solution.py:350
  48.5 2.2 shard_map.324
  50.8 1.8 fusion.30
  55.6 3.5 %fusion.8 = (f32[256,1536]{1,0:T(8,128)}, bf16[256,1536]{1,0:T(8,128)(2,1)S(1)}) fusion(f32[1536]{0:T(1024)S(1)} %reduce.6, bf16[256,768]{1,0:T(8,128)(2,1)} %get-tuple-element.301, bf16[768,1536]{1,0:T(8,128)(2,1)S(1)} %get-tuple-element.161.up), kind=kOutput, calls=%fused_computation.24 | convolution fusion | flops 608305152 | bytes 5117952 | tf_op jit(solution)/shard_map/dot_general | solution.py:22
  64.4 2.3 fusion.12
  69.8 2.0 dynamic-slice_bitcast_fusion
  71.9 2.2 copy.42
  74.1 2.2 copy.43
  80.2 5.4 %shard_map.325 = (f32[256,768]{1,0:T(8,128)S(1)}, f32[256,768]{1,0:T(8,128)S(1)}, bf16[256,768]{1,0:T(8,128)(2,1)S(1)}, bf16[256,1536]{1,0:T(8,128)(2,1)S(1)}, f...) custom-call(f32[256,768]{1,0:T(8,128)S(1)} %copy-done.6, f32[256,768]{1,0:T(8,128)} %fusion.52.part, ...), custom_call_target="tpu_custom_call" | custom-call | flops 1 | bytes 1 | tf_op jit(solution)/shard_map/pallas_call | solution.py:181
  86.7 10.0 %collective-permute-done.7.got = f32[256,768]{1,0:T(8,128)} collective-permute-done((f32[256,768]{1,0:T(8,128)}, f32[256,768]{1,0:T(8,128)}, u32[]{:S(2)}, u32[]{:S(2)}) %collective-permute-start.7) | collective-permute-done | bytes 786464 | tf_op jit(solution)/shard_map/ppermute | solution.py:66
  96.8 5.5 %shard_map.326 = (f32[256,768]{1,0:T(8,128)S(1)}, f32[256,768]{1,0:T(8,128)S(1)}, bf16[256,768]{1,0:T(8,128)(2,1)S(1)}, bf16[256,1536]{1,0:T(8,128)(2,1)S(1)}, f...) custom-call(f32[256,768]{1,0:T(8,128)S(1)} %copy-done.7, f32[256,768]{1,0:T(8,128)} %fusion.53.part, ...), custom_call_target="tpu_custom_call" | custom-call | flops 1 | bytes 1 | tf_op jit(solution)/shard_map/pallas_call | solution.py:181
  102.4 2.2 fusion.54
  104.7 2.3 fusion.55
  107.0 1.8 collective-permute-start.12
  108.9 2.2 fusion.56
  111.1 2.4 collective-permute-done.9.got
  114.6 2.2 fusion.57
  118.0 4.3 %dynamic-slice_add_fusion.2 = (f32[384,768]{1,0:T(8,128)}, f32[384,768]{1,0:T(8,128)}) fusion(f32[768,768]{1,0:T(8,128)} %collective-permute-done.12, s32[]{:T(128)S(6)} %select_n.140, f32[768,768]{1,0:T(8,128)} %fusion.54, s32[]{:T(128)S(6)} %select_n.139), kind=kLoop, calls=%fused_computation.65 | loop fusion | flops 589824 | bytes 7077896 | tf_op jit(solution)/shard_map/add | solution.py:142
  123.1 3.4 %dynamic-slice_add_fusion = (f32[384,768]{1,0:T(8,128)}, f32[384,768]{1,0:T(8,128)}) fusion(f32[768,768]{1,0:T(8,128)} %collective-permute-done.11, s32[]{:T(128)S(6)} %select_n.140, f32[768,768]{1,0:T(8,128)S(1)} %copy-done.52, s32[]{:T(128)S(6)} %select_n.139), kind=kLoop, calls=%fused_computation.63 | loop fusion | flops 589824 | bytes 7077896 | tf_op jit(solution)/shard_map/add | solution.py:142
  131.6 10.4 %collective-permute-done.10.got = f32[256,768]{1,0:T(8,128)} collective-permute-done((f32[256,768]{1,0:T(8,128)S(1)}, f32[256,768]{1,0:T(8,128)}, u32[]{:S(2)}, u32[]{:S(2)}) %collective-permute-start.10) | collective-permute-done | bytes 786464 | tf_op jit(solution)/shard_map/ppermute | solution.py:66
  142.0 2.3 shard_map.328
  148.2 2.4 dynamic-slice_add_fusion.8
  153.3 2.5 dynamic-slice_add_fusion.6
  159.3 10.5 %shard_map.329 = (bf16[3,64,1024]{2,1,0:T(8,128)(2,1)S(1)}, bf16[3,1024,64]{2,1,0:T(8,128)(2,1)S(1)}, bf16[3,1024,64]{2,1,0:T(8,128)(2,1)S(1)}) custom-call(bf16[3,1024,64]{2,1,0:T(8,128)(2,1)S(1)} %bitcast.136, bf16[3,1024,64]{2,1,0:T(8,128)(2,1)S(1)} %copy-done.11, bf16[3,1024,64]{2,1,0:T(8,128)(2,1)S(1)} %bitcast.137, f32[3,1,1024]{2,1,0:T(1,128)S(1)} %add.341.sums, ...), custom_call_target="tpu_custom_call" | custom-call | flops 1 | bytes 1 | tf_op jit(solution)/shard_map/pallas_call | solution.py:181
  176.8 2.2 select_bitcast_fusion.3
  181.3 1.9 collective-permute-start.22
  184.4 3.7 %collective-permute-done.20 = f32[192,768]{1,0:T(8,128)S(1)} collective-permute-done((f32[192,768]{1,0:T(8,128)S(1)}, f32[192,768]{1,0:T(8,128)S(1)}, u32[]{:S(2)}, u32[]{:S(2)}) %collective-permute-start.20) | collective-permute-done | bytes 589856 | tf_op jit(solution)/shard_map/ppermute | solution.py:66
  191.6 10.6 %collective-permute-done.18 = f32[256,768]{1,0:T(8,128)S(1)} collective-permute-done((f32[256,768]{1,0:T(8,128)S(1)}, f32[256,768]{1,0:T(8,128)S(1)}, u32[]{:S(2)}, u32[]{:S(2)}) %collective-permute-start.18) | collective-permute-done | bytes 786464 | tf_op jit(solution)/shard_map/ppermute | solution.py:66
  202.4 7.5 %collective-permute-done.22 = f32[192,768]{1,0:T(8,128)S(1)} collective-permute-done((f32[192,768]{1,0:T(8,128)S(1)}, f32[192,768]{1,0:T(8,128)S(1)}, u32[]{:S(2)}, u32[]{:S(2)}) %collective-permute-start.22) | collective-permute-done | bytes 589856 | tf_op jit(solution)/shard_map/ppermute | solution.py:66
  216.9 3.2 %collective-permute-done.23 = f32[192,768]{1,0:T(8,128)} collective-permute-done((f32[192,768]{1,0:T(8,128)}, f32[192,768]{1,0:T(8,128)}, u32[]{:S(2)}, u32[]{:S(2)}) %collective-permute-start.23) | collective-permute-done | bytes 589856 | tf_op jit(solution)/shard_map/ppermute | solution.py:66
  222.6 10.4 %collective-permute-done.21 = f32[256,768]{1,0:T(8,128)} collective-permute-done((f32[256,768]{1,0:T(8,128)S(1)}, f32[256,768]{1,0:T(8,128)}, u32[]{:S(2)}, u32[]{:S(2)}) %collective-permute-start.21) | collective-permute-done | bytes 786464 | tf_op jit(solution)/shard_map/ppermute | solution.py:66
  235.5 6.9 %collective-permute-done.28 = f32[192,768]{1,0:T(8,128)S(1)} collective-permute-done((f32[192,768]{1,0:T(8,128)}, f32[192,768]{1,0:T(8,128)S(1)}, u32[]{:S(2)}, u32[]{:S(2)}) %collective-permute-start.28) | collective-permute-done | bytes 589856 | tf_op jit(solution)/shard_map/ppermute | solution.py:66
  243.8 2.2 collective-permute-start.33
  246.0 7.5 %collective-permute-start.26 = (f32[1,6144]{1,0:T(1,128)S(1)}, f32[1,6144]{1,0:T(1,128)S(1)}, u32[]{:S(2)}, u32[]{:S(2)}) collective-permute-start(f32[1,6144]{1,0:T(1,128)S(1)} %bitcast.163), channel_id=1, source_target_pairs={{0,1},{1,0},{2,3},{3,2},{4,5},{5,4},{6,7},{7,6},{8,9},{9,8},{10,11... | collective-permute-start | bytes 73736 | tf_op jit(solution)/shard_map/ppermute | solution.py:66
  257.7 7.7 %collective-permute-done.33 = f32[192,768]{1,0:T(8,128)} collective-permute-done((f32[192,768]{1,0:T(8,128)S(1)}, f32[192,768]{1,0:T(8,128)}, u32[]{:S(2)}, u32[]{:S(2)}) %collective-permute-start.33) | collective-permute-done | bytes 589856 | tf_op jit(solution)/shard_map/ppermute | solution.py:66
  267.0 5.0 %collective-permute-done.32 = f32[384,768]{1,0:T(8,128)} collective-permute-done((f32[384,768]{1,0:T(8,128)}, f32[384,768]{1,0:T(8,128)}, u32[]{:S(2)}, u32[]{:S(2)}) %collective-permute-start.32) | collective-permute-done | bytes 1179680 | tf_op jit(solution)/shard_map/ppermute | solution.py:66
  271.9 1.8 broadcast_select_fusion.5
  275.2 14.1 %collective-permute-done.31 = f32[1,6528]{1,0:T(1,128)S(1)} collective-permute-done((f32[1,6528]{1,0:T(1,128)S(1)}, f32[1,6528]{1,0:T(1,128)S(1)}, u32[]{:S(2)}, u32[]{:S(2)}) %collective-permute-start.31) | collective-permute-done | bytes 26144 | tf_op jit(solution)/shard_map/ppermute | solution.py:66
  289.4 2.7 collective-permute-start.34
  294.1 2.3 collective-permute-start.36
  300.8 9.2 %collective-permute-done.36 = f32[384,768]{1,0:T(8,128)S(1)} collective-permute-done((f32[384,768]{1,0:T(8,128)S(1)}, f32[384,768]{1,0:T(8,128)S(1)}, u32[]{:S(2)}, u32[]{:S(2)}) %collective-permute-start.36) | collective-permute-done | bytes 1179680 | tf_op jit(solution)/shard_map/ppermute | solution.py:66
  (368 shorter events, 95.3 us)
Async XLA Ops:
  7.2 35.4 %all-gather.2.cloned.1.call-start = ((), (), s32[]{:S(2)}) async-start(), calls=%async_computation | async-start | bytes 2949120 | tf_op jit(solution)/shard_map/all_gather | solution.py:350
  10.2 25.3 %collective-permute-start.2 = (f32[768,768]{1,0:T(8,128)}, f32[768,768]{1,0:T(8,128)}, u32[]{:S(2)}, u32[]{:S(2)}) collective-permute-start(f32[768,768]{1,0:T(8,128)} %convert_multiply_fusion.1), channel_id=1, source_target_pairs={{0,1},{1,0},{2,3},{3,2},{4,5},{5,4},{6,7},{7,6},{8,9},{9,8},{10,11... | collective-permute-start | bytes 7077896 | tf_op jit(solution)/shard_map/ppermute | solution.py:66
  11.8 23.7 %collective-permute-start.3 = (f32[768,768]{1,0:T(8,128)}, f32[768,768]{1,0:T(8,128)S(1)}, u32[]{:S(2)}, u32[]{:S(2)}) collective-permute-start(f32[768,768]{1,0:T(8,128)} %convert_multiply_fusion), channel_id=1, source_target_pairs={{0,1},{1,0},{2,3},{3,2},{4,5},{5,4},{6,7},{7,6},{8,9},{9,8},{10,11... | collective-permute-start | bytes 7077896 | tf_op jit(solution)/shard_map/ppermute | solution.py:66
  28.6 2.0 collective-permute-start
  31.7 19.1 %collective-permute-start.1 = (f32[256,384]{1,0:T(8,128)}, f32[256,384]{1,0:T(8,128)}, u32[]{:S(2)}, u32[]{:S(2)}) collective-permute-start(f32[256,384]{1,0:T(8,128)} %get-tuple-element.154), channel_id=1, source_target_pairs={{0,2},{1,3},{2,0},{3,1},{4,6},{5,7},{6,4},{7,5},{8,10},{9,11},{10,... | collective-permute-start | bytes 1179656 | tf_op jit(solution)/shard_map/ppermute | solution.py:66
  34.0 8.6 %collective-permute-start.4 = (f32[1,768]{1,0:T(1,128)S(1)}, f32[1,768]{1,0:T(1,128)S(1)}, u32[]{:S(2)}, u32[]{:S(2)}) collective-permute-start(f32[1,768]{1,0:T(1,128)S(1)} %reshape.385.bias), channel_id=1, source_target_pairs={{0,1},{1,0},{2,3},{3,2},{4,5},{5,4},{6,7},{7,6},{8,9},{9,8},{10,11... | collective-permute-start | bytes 9224 | tf_op jit(solution)/shard_map/ppermute | solution.py:66
  35.4 25.3 %collective-permute-start.6 = (f32[256,384]{1,0:T(8,128)}, f32[256,384]{1,0:T(8,128)}, u32[]{:S(2)}, u32[]{:S(2)}) collective-permute-start(f32[256,384]{1,0:T(8,128)} %get-tuple-element.155), channel_id=1, source_target_pairs={{0,2},{1,3},{2,0},{3,1},{4,6},{5,7},{6,4},{7,5},{8,10},{9,11},{10,... | collective-permute-start | bytes 1179656 | tf_op jit(solution)/shard_map/ppermute | solution.py:66
  60.7 19.2 %collective-permute-start.5 = (f32[256,768]{1,0:T(8,128)}, f32[256,768]{1,0:T(8,128)}, u32[]{:S(2)}, u32[]{:S(2)}) collective-permute-start(f32[256,768]{1,0:T(8,128)} %fusion.52.part), channel_id=1, source_target_pairs={{0,2},{1,3},{2,0},{3,1},{4,6},{5,7},{6,4},{7,5},{8,10},{9,11},{10,... | collective-permute-start | bytes 2359304 | tf_op jit(solution)/shard_map/ppermute | solution.py:66
  68.4 28.3 %collective-permute-start.7 = (f32[256,768]{1,0:T(8,128)}, f32[256,768]{1,0:T(8,128)}, u32[]{:S(2)}, u32[]{:S(2)}) collective-permute-start(f32[256,768]{1,0:T(8,128)} %fusion.53.part), channel_id=1, source_target_pairs={{0,2},{1,3},{2,0},{3,1},{4,6},{5,7},{6,4},{7,5},{8,10},{9,11},{10,... | collective-permute-start | bytes 2359304 | tf_op jit(solution)/shard_map/ppermute | solution.py:66
  79.4 34.1 %copy-start.14 = (bf16[192,768]{1,0:T(8,128)(2,1)}, bf16[192,768]{1,0:T(8,128)(2,1)S(1)}, u32[]{:S(2)}) copy-start(bf16[192,768]{1,0:T(8,128)(2,1)S(1)} %get-tuple-element.353.pair) | copy-start | bytes 884740
  79.4 34.1 %copy-start.16 = (bf16[192,768]{1,0:T(8,128)(2,1)}, bf16[192,768]{1,0:T(8,128)(2,1)S(1)}, u32[]{:S(2)}) copy-start(bf16[192,768]{1,0:T(8,128)(2,1)S(1)} %get-tuple-element.354.own) | copy-start | bytes 884740
  80.2 16.6 %copy-start.7 = (f32[256,768]{1,0:T(8,128)S(1)}, f32[256,768]{1,0:T(8,128)}, u32[]{:S(2)}) copy-start(f32[256,768]{1,0:T(8,128)} %get-tuple-element.299.hidden) | copy-start | bytes 2359300
  80.2 16.6 %copy-start.25 = (bf16[256,768]{1,0:T(8,128)(2,1)S(1)}, bf16[256,768]{1,0:T(8,128)(2,1)}, u32[]{:S(2)}) copy-start(bf16[256,768]{1,0:T(8,128)(2,1)} %get-tuple-element.339.cotangent) | copy-start | bytes 1179652
  80.2 16.6 %copy-start.28 = (f32[256,1536]{1,0:T(8,128)S(1)}, f32[256,1536]{1,0:T(8,128)}, u32[]{:S(2)}) copy-start(f32[256,1536]{1,0:T(8,128)} %get-tuple-element.337.slope) | copy-start | bytes 4718596
  86.6 26.9 %collective-permute-start.9 = (f32[256,768]{1,0:T(8,128)S(1)}, f32[256,768]{1,0:T(8,128)S(1)}, u32[]{:S(2)}, u32[]{:S(2)}) collective-permute-start(f32[256,768]{1,0:T(8,128)S(1)} %get-tuple-element.190.part), channel_id=1, source_target_pairs={{0,2},{1,3},{2,0},{3,1},{4,6},{5,7},{6,4},{7,5},{8,10},{9,11},{10,... | collective-permute-start | bytes 2359304 | tf_op jit(solution)/shard_map/ppermute | solution.py:66
  107.0 11.0 %collective-permute-start.12 = (f32[768,768]{1,0:T(8,128)}, f32[768,768]{1,0:T(8,128)}, u32[]{:S(2)}, u32[]{:S(2)}) collective-permute-start(f32[768,768]{1,0:T(8,128)} %fusion.55), channel_id=1, source_target_pairs={{0,1},{1,0},{2,3},{3,2},{4,5},{5,4},{6,7},{7,6},{8,9},{9,8},{10,11... | collective-permute-start | bytes 7077896 | tf_op jit(solution)/shard_map/ppermute | solution.py:66
  116.8 6.2 %collective-permute-start.11 = (f32[768,768]{1,0:T(8,128)}, f32[768,768]{1,0:T(8,128)}, u32[]{:S(2)}, u32[]{:S(2)}) collective-permute-start(f32[768,768]{1,0:T(8,128)} %fusion.57), channel_id=1, source_target_pairs={{0,1},{1,0},{2,3},{3,2},{4,5},{5,4},{6,7},{7,6},{8,9},{9,8},{10,11... | collective-permute-start | bytes 7077896 | tf_op jit(solution)/shard_map/ppermute | solution.py:66
  122.3 25.9 %collective-permute-start.15 = (f32[384,768]{1,0:T(8,128)}, f32[384,768]{1,0:T(8,128)}, u32[]{:S(2)}, u32[]{:S(2)}) collective-permute-start(f32[384,768]{1,0:T(8,128)} %get-tuple-element.307), channel_id=1, source_target_pairs={{0,4},{1,9},{2,6},{3,11},{4,0},{5,13},{6,2},{7,15},{8,12},{9,1},{1... | collective-permute-start | bytes 3538952 | tf_op jit(solution)/shard_map/ppermute | solution.py:66
  123.1 18.9 %collective-permute-start.10 = (f32[256,768]{1,0:T(8,128)S(1)}, f32[256,768]{1,0:T(8,128)}, u32[]{:S(2)}, u32[]{:S(2)}) collective-permute-start(f32[256,768]{1,0:T(8,128)S(1)} %copy-done.41), channel_id=1, source_target_pairs={{0,2},{1,3},{2,0},{3,1},{4,6},{5,7},{6,4},{7,5},{8,10},{9,11},{10,... | collective-permute-start | bytes 2359304 | tf_op jit(solution)/shard_map/ppermute | solution.py:66
  123.1 18.8 %copy-start.39 = (f32[256,768]{1,0:T(8,128)S(1)}, f32[256,768]{1,0:T(8,128)}, u32[]{:S(2)}) copy-start(f32[256,768]{1,0:T(8,128)} %copy-done.38) | copy-start | bytes 2359300
  126.5 15.4 %copy-start.12 = (f32[256,768]{1,0:T(8,128)S(1)}, f32[256,768]{1,0:T(8,128)}, u32[]{:S(2)}) copy-start(f32[256,768]{1,0:T(8,128)} %get-tuple-element.300.normed) | copy-start | bytes 2359300
  126.5 15.4 %copy-start.15 = (bf16[192,768]{1,0:T(8,128)(2,1)S(1)}, bf16[192,768]{1,0:T(8,128)(2,1)}, u32[]{:S(2)}) copy-start(bf16[192,768]{1,0:T(8,128)(2,1)} %copy-done.14) | copy-start | bytes 884740
  126.5 15.4 %copy-start.17 = (bf16[192,768]{1,0:T(8,128)(2,1)S(1)}, bf16[192,768]{1,0:T(8,128)(2,1)}, u32[]{:S(2)}) copy-start(bf16[192,768]{1,0:T(8,128)(2,1)} %copy-done.16) | copy-start | bytes 884740
  126.5 26.8 %collective-permute-start.14 = (f32[384,768]{1,0:T(8,128)}, f32[384,768]{1,0:T(8,128)}, u32[]{:S(2)}, u32[]{:S(2)}) collective-permute-start(f32[384,768]{1,0:T(8,128)} %get-tuple-element.305), channel_id=1, source_target_pairs={{0,4},{1,9},{2,6},{3,11},{4,0},{5,13},{6,2},{7,15},{8,12},{9,1},{1... | collective-permute-start | bytes 3538952 | tf_op jit(solution)/shard_map/ppermute | solution.py:66
  144.4 7.4 %collective-permute-start.13 = (f32[512,192]{1,0:T(8,128)S(1)}, f32[512,192]{1,0:T(8,128)S(1)}, u32[]{:S(2)}, u32[]{:S(2)}) collective-permute-start(f32[512,192]{1,0:T(8,128)S(1)} %pad_maximum_fusion.13), channel_id=1, source_target_pairs={{0,1},{1,0},{2,3},{3,2},{4,5},{5,4},{6,7},{7,6},{8,9},{9,8},{10,11... | collective-permute-start | bytes 1179656 | tf_op jit(solution)/shard_map/ppermute | solution.py:66
  147.5 29.2 %collective-permute-start.8 = (f32[512,768]{1,0:T(8,128)}, f32[512,768]{1,0:T(8,128)}, u32[]{:S(2)}, u32[]{:S(2)}) collective-permute-start(f32[512,768]{1,0:T(8,128)} %constant_dynamic-update-slice_fusion), channel_id=1, source_target_pairs={{0,1},{1,0},{2,3},{3,2},{4,5},{5,4},{6,7},{7,6},{8,9},{9,8},{10,11... | collective-permute-start | bytes 4718600 | tf_op jit(solution)/shard_map/ppermute | solution.py:66
  150.6 23.4 %collective-permute-start.16 = (f32[192,768]{1,0:T(8,128)}, f32[192,768]{1,0:T(8,128)}, u32[]{:S(2)}, u32[]{:S(2)}) collective-permute-start(f32[192,768]{1,0:T(8,128)} %get-tuple-element.325), channel_id=1, source_target_pairs={{0,8},{1,5},{2,10},{3,7},{4,12},{5,1},{6,14},{7,3},{8,0},{9,13},{1... | collective-permute-start | bytes 1769480 | tf_op jit(solution)/shard_map/ppermute | solution.py:66
  176.3 3.5 %collective-permute-start.17 = (f32[512,768]{1,0:T(8,128)S(1)}, f32[512,768]{1,0:T(8,128)S(1)}, u32[]{:S(2)}, u32[]{:S(2)}) collective-permute-start(f32[512,768]{1,0:T(8,128)S(1)} %fusion.24), channel_id=1, source_target_pairs={{0,1},{1,0},{2,3},{3,2},{4,5},{5,4},{6,7},{7,6},{8,9},{9,8},{10,11... | collective-permute-start | bytes 4718600 | tf_op jit(solution)/shard_map/ppermute | solution.py:66
  179.0 9.1 %collective-permute-start.20 = (f32[192,768]{1,0:T(8,128)S(1)}, f32[192,768]{1,0:T(8,128)S(1)}, u32[]{:S(2)}, u32[]{:S(2)}) collective-permute-start(f32[192,768]{1,0:T(8,128)S(1)} %copy-done.69), channel_id=1, source_target_pairs={{0,8},{1,5},{2,10},{3,7},{4,12},{5,1},{6,14},{7,3},{8,0},{9,13},{1... | collective-permute-start | bytes 1769480 | tf_op jit(solution)/shard_map/ppermute | solution.py:66
  180.4 8.6 %collective-permute-start.19 = (f32[192,768]{1,0:T(8,128)S(1)}, f32[192,768]{1,0:T(8,128)S(1)}, u32[]{:S(2)}, u32[]{:S(2)}) collective-permute-start(f32[192,768]{1,0:T(8,128)S(1)} %fusion.58), channel_id=1, source_target_pairs={{0,1},{1,0},{2,3},{3,2},{4,5},{5,4},{6,7},{7,6},{8,9},{9,8},{10,11... | collective-permute-start | bytes 1769480 | tf_op jit(solution)/shard_map/ppermute | solution.py:66
  181.3 28.6 %collective-permute-start.22 = (f32[192,768]{1,0:T(8,128)S(1)}, f32[192,768]{1,0:T(8,128)S(1)}, u32[]{:S(2)}, u32[]{:S(2)}) collective-permute-start(f32[192,768]{1,0:T(8,128)S(1)} %add.358), channel_id=1, source_target_pairs={{0,16},{1,17},{2,18},{3,19},{4,20},{5,21},{6,22},{7,23},{8,24},{9,... | collective-permute-start | bytes 1769480 | tf_op jit(solution)/shard_map/ppermute | solution.py:66
  183.3 18.9 %collective-permute-start.18 = (f32[256,768]{1,0:T(8,128)S(1)}, f32[256,768]{1,0:T(8,128)S(1)}, u32[]{:S(2)}, u32[]{:S(2)}) collective-permute-start(f32[256,768]{1,0:T(8,128)S(1)} %add.359), channel_id=1, source_target_pairs={{0,2},{1,3},{2,0},{3,1},{4,6},{5,7},{6,4},{7,5},{8,10},{9,11},{10,... | collective-permute-start | bytes 2359304 | tf_op jit(solution)/shard_map/ppermute | solution.py:66
  190.8 23.3 %collective-permute-start.24 = (f32[384,768]{1,0:T(8,128)}, f32[384,768]{1,0:T(8,128)}, u32[]{:S(2)}, u32[]{:S(2)}) collective-permute-start(f32[384,768]{1,0:T(8,128)} %get-tuple-element.321), channel_id=1, source_target_pairs={{0,4},{1,9},{2,6},{3,11},{4,0},{5,13},{6,2},{7,15},{8,12},{9,1},{1... | collective-permute-start | bytes 3538952 | tf_op jit(solution)/shard_map/ppermute | solution.py:66
  210.8 9.3 %collective-permute-start.23 = (f32[192,768]{1,0:T(8,128)}, f32[192,768]{1,0:T(8,128)}, u32[]{:S(2)}, u32[]{:S(2)}) collective-permute-start(f32[192,768]{1,0:T(8,128)} %add.365), channel_id=1, source_target_pairs={{0,8},{1,5},{2,10},{3,7},{4,12},{5,1},{6,14},{7,3},{8,0},{9,13},{1... | collective-permute-start | bytes 1769480 | tf_op jit(solution)/shard_map/ppermute | solution.py:66
  213.4 19.5 %collective-permute-start.21 = (f32[256,768]{1,0:T(8,128)S(1)}, f32[256,768]{1,0:T(8,128)}, u32[]{:S(2)}, u32[]{:S(2)}) collective-permute-start(f32[256,768]{1,0:T(8,128)S(1)} %add.360), channel_id=1, source_target_pairs={{0,2},{1,3},{2,0},{3,1},{4,6},{5,7},{6,4},{7,5},{8,10},{9,11},{10,... | collective-permute-start | bytes 2359304 | tf_op jit(solution)/shard_map/ppermute | solution.py:66
  214.0 28.4 %collective-permute-start.28 = (f32[192,768]{1,0:T(8,128)}, f32[192,768]{1,0:T(8,128)S(1)}, u32[]{:S(2)}, u32[]{:S(2)}) collective-permute-start(f32[192,768]{1,0:T(8,128)} %add.361), channel_id=1, source_target_pairs={{0,16},{1,17},{2,18},{3,19},{4,20},{5,21},{6,22},{7,23},{8,24},{9,... | collective-permute-start | bytes 1769480 | tf_op jit(solution)/shard_map/ppermute | solution.py:66
  215.8 27.9 %collective-permute-start.27 = (f32[192,768]{1,0:T(8,128)S(1)}, f32[192,768]{1,0:T(8,128)S(1)}, u32[]{:S(2)}, u32[]{:S(2)}) collective-permute-start(f32[192,768]{1,0:T(8,128)S(1)} %get-tuple-element.319), channel_id=1, source_target_pairs={{0,8},{1,5},{2,10},{3,7},{4,12},{5,1},{6,14},{7,3},{8,0},{9,13},{1... | collective-permute-start | bytes 1769480 | tf_op jit(solution)/shard_map/ppermute | solution.py:66
  222.6 49.3 %collective-permute-start.32 = (f32[384,768]{1,0:T(8,128)}, f32[384,768]{1,0:T(8,128)}, u32[]{:S(2)}, u32[]{:S(2)}) collective-permute-start(f32[384,768]{1,0:T(8,128)} %pad_maximum_fusion.8), channel_id=1, source_target_pairs={{0,4},{1,9},{2,6},{3,11},{4,0},{5,13},{6,2},{7,15},{8,12},{9,1},{1... | collective-permute-start | bytes 3538952 | tf_op jit(solution)/shard_map/ppermute | solution.py:66
  242.5 12.0 %collective-permute-start.30 = (f32[192,768]{1,0:T(8,128)S(1)}, f32[192,768]{1,0:T(8,128)}, u32[]{:S(2)}, u32[]{:S(2)}) collective-permute-start(f32[192,768]{1,0:T(8,128)S(1)} %add.384), channel_id=1, source_target_pairs={{0,8},{1,5},{2,10},{3,7},{4,12},{5,1},{6,14},{7,3},{8,0},{9,13},{1... | collective-permute-start | bytes 1769480 | tf_op jit(solution)/shard_map/ppermute | solution.py:66
  242.9 49.2 %collective-permute-start.25 = (f32[512,768]{1,0:T(8,128)}, f32[512,768]{1,0:T(8,128)}, u32[]{:S(2)}, u32[]{:S(2)}) collective-permute-start(f32[512,768]{1,0:T(8,128)} %pad_maximum_fusion.6), channel_id=1, source_target_pairs={{0,1},{1,0},{2,3},{3,2},{4,5},{5,4},{6,7},{7,6},{8,9},{9,8},{10,11... | collective-permute-start | bytes 4718600 | tf_op jit(solution)/shard_map/ppermute | solution.py:66
  243.8 21.6 %collective-permute-start.33 = (f32[192,768]{1,0:T(8,128)S(1)}, f32[192,768]{1,0:T(8,128)}, u32[]{:S(2)}, u32[]{:S(2)}) collective-permute-start(f32[192,768]{1,0:T(8,128)S(1)} %add.385), channel_id=1, source_target_pairs={{0,16},{1,17},{2,18},{3,19},{4,20},{5,21},{6,22},{7,23},{8,24},{9,... | collective-permute-start | bytes 1769480 | tf_op jit(solution)/shard_map/ppermute | solution.py:66
  246.0 8.3 %collective-permute-start.26 = (f32[1,6144]{1,0:T(1,128)S(1)}, f32[1,6144]{1,0:T(1,128)S(1)}, u32[]{:S(2)}, u32[]{:S(2)}) collective-permute-start(f32[1,6144]{1,0:T(1,128)S(1)} %bitcast.163), channel_id=1, source_target_pairs={{0,1},{1,0},{2,3},{3,2},{4,5},{5,4},{6,7},{7,6},{8,9},{9,8},{10,11... | collective-permute-start | bytes 73736 | tf_op jit(solution)/shard_map/ppermute | solution.py:66
  254.5 3.1 collective-permute-start.29
  255.8 42.1 %collective-permute-start.37 = (f32[384,768]{1,0:T(8,128)S(1)}, f32[384,768]{1,0:T(8,128)S(1)}, u32[]{:S(2)}, u32[]{:S(2)}) collective-permute-start(f32[384,768]{1,0:T(8,128)S(1)} %pad_maximum_fusion.9), channel_id=1, source_target_pairs={{0,4},{1,9},{2,6},{3,11},{4,0},{5,13},{6,2},{7,15},{8,12},{9,1},{1... | collective-permute-start | bytes 3538952 | tf_op jit(solution)/shard_map/ppermute | solution.py:66
  257.6 31.7 %collective-permute-start.31 = (f32[1,6528]{1,0:T(1,128)S(1)}, f32[1,6528]{1,0:T(1,128)S(1)}, u32[]{:S(2)}, u32[]{:S(2)}) collective-permute-start(f32[1,6528]{1,0:T(1,128)S(1)} %add.387), channel_id=1, source_target_pairs={{0,8},{1,9},{2,10},{3,11},{4,12},{5,13},{6,14},{7,15},{8,0},{9,1},... | collective-permute-start | bytes 78344 | tf_op jit(solution)/shard_map/ppermute | solution.py:66
  266.6 27.4 %collective-permute-start.35 = (f32[192,768]{1,0:T(8,128)S(1)}, f32[192,768]{1,0:T(8,128)S(1)}, u32[]{:S(2)}, u32[]{:S(2)}) collective-permute-start(f32[192,768]{1,0:T(8,128)S(1)} %add.388), channel_id=1, source_target_pairs={{0,8},{1,5},{2,10},{3,7},{4,12},{5,1},{6,14},{7,3},{8,0},{9,13},{1... | collective-permute-start | bytes 1769480 | tf_op jit(solution)/shard_map/ppermute | solution.py:66
  289.4 8.4 %collective-permute-start.34 = (f32[1,6528]{1,0:T(1,128)S(1)}, f32[1,6528]{1,0:T(1,128)S(1)}, u32[]{:S(2)}, u32[]{:S(2)}) collective-permute-start(f32[1,6528]{1,0:T(1,128)S(1)} %add.389), channel_id=1, source_target_pairs={{0,16},{1,17},{2,18},{3,19},{4,20},{5,21},{6,22},{7,23},{8,24},{9,... | collective-permute-start | bytes 78344 | tf_op jit(solution)/shard_map/ppermute | solution.py:66
  294.1 15.9 %collective-permute-start.36 = (f32[384,768]{1,0:T(8,128)S(1)}, f32[384,768]{1,0:T(8,128)S(1)}, u32[]{:S(2)}, u32[]{:S(2)}) collective-permute-start(f32[384,768]{1,0:T(8,128)S(1)} %pad_maximum_fusion.10), channel_id=1, source_target_pairs={{0,4},{1,9},{2,6},{3,11},{4,0},{5,13},{6,2},{7,15},{8,12},{9,1},{1... | collective-permute-start | bytes 3538952 | tf_op jit(solution)/shard_map/ppermute | solution.py:66
  (83 other events, 260.2 us)
Sparse Core Ops, SparseCore 0:
  13.2 29.3 all-gather.1
